TPU v7x, 32 devices: a whole 2x2x4 slice. The times are simulated.
32 devices in a mesh: grp: 4 (over y, x), lm: 8 (over z, core).
Axes of the slice: x: 2, y: 2, z: 4, core: 2. Of those that a mesh axis runs over, the one named last changes fastest.
Arguments:
- embeddings: bfloat16 [8192, 512], P(('grp', 'lm')), may hold values from -14 to 14
- landmarks: bfloat16 [16384, 512], P('lm'), may hold values from -14 to 14
- start_vectors: float32 [8192, 128], P(('grp', 'lm')), may hold values from -10 to 10
- row_weight: float32 [8192], P(('grp', 'lm')), may hold values from 0.1 to 9
- spread: float32 [1], replicated, may hold values from 11.313708 to 33.941124
Outputs:
- subspace: float32 [8192, 128], P(('grp', 'lm'))
All inputs are finite; a program needn't handle non-finite values.
Results may differ from a plain program's by a relative error of at most 0.019.
Values may be sent and summed in bfloat16 or wider, within the bound.
A program may use at most 128 MiB of HBM per device.

v0:
```python
import functools

import jax
import jax.numpy as jnp
from jax import lax
from jax.experimental import pallas as pl
from jax.experimental.pallas import tpu as pltpu
from jax.sharding import PartitionSpec as P

ITERS = 2
F32 = jnp.float32
BF16 = jnp.bfloat16
BUILD = 1024
HIGHEST = lax.Precision.HIGHEST


def nt(a, b):
    return lax.dot_general(a, b, (((1,), (1,)), ((), ())), preferred_element_type=F32)


def nn(a, b):
    return jnp.dot(a, b, preferred_element_type=F32)


def tile(total, most):
    size = min(total, most)
    while total % size:
        size -= 8
    return size


def rows_at(index, size):
    return pl.ds(pl.multiple_of(index * size, size), size)


def kernel(
    groups, members, spread_ref, emb_ref, marks_ref, vec_ref, weight_ref, out_ref,
    marks_in, marks_unit, kern_t, unit, weighted, stats, side, means,
    side_out, side_in, side_stats_out, side_stats, side_b, shifts,
    image_out, pair_in, line_out, line_in, norms, group_norms,
    row_sems, stat_sems, grp_sems, img_sems, norm_sems, mark_sems,
):
    own, width = emb_ref.shape
    marks = marks_ref.shape[0]
    vecs = vec_ref.shape[1]
    part = marks // groups
    line = members // 2
    total_rows = own * groups * members
    me_g = lax.axis_index("grp")
    me_l = lax.axis_index("lm")
    z = me_l // 2
    c = me_l % 2
    sends = []
    half = own // 2

    def to(src, dst, send_sem, recv_sem, when=None, **device):
        copy = pltpu.make_async_remote_copy(
            src_ref=src, dst_ref=dst, send_sem=send_sem, recv_sem=recv_sem,
            device_id=device, device_id_type=pl.DeviceIdType.MESH,
        )
        if when is None:
            copy.start()
        else:
            pl.when(when)(copy.start)
        sends.append((when, copy))

    def arrived(ref, sem):
        pltpu.make_async_remote_copy(
            src_ref=ref, dst_ref=ref, send_sem=sem, recv_sem=sem,
            device_id={"lm": me_l}, device_id_type=pl.DeviceIdType.MESH,
        ).wait_recv()

    def mate():
        return z * 2 + 1 - c

    def along(k):
        return (z + k) % line * 2 + c

    def group(j):
        return (me_g + j) % groups

    order = sorted(range(1, line), key=lambda k: min(k, line - k))

    barrier = pltpu.get_barrier_semaphore()
    for k in range(1, members):
        pl.semaphore_signal(
            barrier, inc=1, device_id={"lm": (me_l + k) % members},
            device_id_type=pl.DeviceIdType.MESH,
        )
    for j in range(1, groups):
        pl.semaphore_signal(
            barrier, inc=1, device_id={"grp": group(j)}, device_id_type=pl.DeviceIdType.MESH
        )

    mark_copies = []
    for j in range(groups):
        mark_copies.append(pltpu.make_async_copy(
            marks_ref.at[pl.ds(pl.multiple_of(group(j) * part, part), part), :],
            marks_in.at[pl.ds(j * part, part), :], mark_sems.at[j],
        ))
        mark_copies[j].start()

    gamma = spread_ref[0]
    weight_row = weight_ref[...]
    weight = jnp.transpose(jnp.broadcast_to(weight_row, (128, own)))[:, :1]
    values = emb_ref[...].astype(F32)
    scale = lax.rsqrt(jnp.sum(values * values, axis=1, keepdims=True) + 1e-06)
    unit[0] = (values * scale).astype(BF16)
    pl.semaphore_wait(barrier, members - 1 + groups - 1)

    def chunk(step, slot):
        pieces = [
            (weighted.at[step, pl.ds(slot * own, own), :], row_sems.at[step, 1]),
            (stats.at[step, slot], row_sems.at[step, 2]),
        ]
        if step == 0:
            pieces = [
                (unit.at[slot, pl.ds(0, half), :], row_sems.at[step, 0]),
                (unit.at[slot, pl.ds(half, half), :], row_sems.at[step, 3]),
            ] + pieces
        return pieces

    def chunk_at(slot):
        return [
            (unit.at[slot, pl.ds(0, half), :], row_sems.at[0, 0]),
            (unit.at[slot, pl.ds(half, half), :], row_sems.at[0, 3]),
            (weighted.at[0, pl.ds(pl.multiple_of(slot * own, own), own), :], row_sems.at[0, 1]),
            (stats.at[0, slot], row_sems.at[0, 2]),
        ]

    def send_own(low, high):
        for right in (1, 0):
            slot = line - 1 if right else 1
            pieces = zip(chunk(0, 0)[low:high], chunk(0, slot)[low:high])
            for (src, sem), (dst, _) in pieces:
                to(
                    src, dst, sem.at[1, right * line], sem.at[0, slot],
                    when=z < line - 1 if right else z > 0,
                    lm=(z + 1 if right else z - 1) * 2 + c,
                )
        for (src, sem), (dst, _) in zip(chunk(0, 0)[low:high], chunk(0, line)[low:high]):
            to(src, dst, sem.at[2, 0], sem.at[0, line], lm=mate())

    def next_slot(t):
        both = jnp.minimum(z, line - 1 - z)
        near = t < 2 * both
        far = jnp.where(near, t // 2 + 1, t - both + 1)
        left = jnp.where(near, t % 2, jnp.where(2 * z < line - 1, 1, 0)) == 0
        return jnp.where(left, line - far, far), left

    def relay(t):
        slot, left = next_slot(t)
        beyond = jnp.where(left, slot - 1, slot + 1)
        more = jnp.where(left, z < line - 1, z > 0)
        follow = jnp.where(more, beyond, slot)
        for (src, sem), (dst, _) in zip(chunk_at(slot), chunk_at(follow)):
            arrived(src, sem.at[0, slot])
            to(
                src, dst, sem.at[1, slot + jnp.where(left, line, 0)], sem.at[0, follow],
                when=more, lm=jnp.where(left, z + 1, z - 1) % line * 2 + c,
            )
        for (src, sem), (dst, _) in zip(chunk_at(slot), chunk_at(line + slot)):
            to(src, dst, sem.at[2, slot], sem.at[0, line + slot], lm=mate())
        return slot

    def spread_chunk(step):
        for (src, sem), (dst, _) in zip(chunk(step, 0), chunk(step, line)):
            to(src, dst, sem.at[1, 0], sem.at[0, line], lm=mate())
        for k in order:
            back = line - k
            for (src, sem), (dst, _) in zip(chunk(step, 0), chunk(step, back)):
                to(src, dst, sem.at[1, k], sem.at[0, back], lm=along(k))

    def pass_on(step, k):
        for (src, sem), (dst, _) in zip(chunk(step, k), chunk(step, line + k)):
            to(src, dst, sem.at[1, line + k], sem.at[0, line + k], lm=mate())

    def await_chunk(step, slot):
        for ref, sem in chunk(step, slot):
            arrived(ref, sem.at[0, slot])

    send_own(0, 2)
    full = weight * vec_ref[...]
    weighted[0, 0:own, :] = full.astype(BF16)
    stats[0, 0] = jnp.zeros(stats.shape[2:], F32)
    stats[0, 0, 0:1, 0:own] = weight_row
    stats[0, 0, 1:2, 0:vecs] = jnp.sum(full, axis=0, keepdims=True)

    send_own(2, 4)

    mark_tile = tile(part, 256)

    def unit_marks(i, carry):
        at = rows_at(i, mark_tile)
        block = marks_in[at, :].astype(F32)
        factor = lax.rsqrt(jnp.sum(block * block, axis=1, keepdims=True) + 1e-06)
        marks_unit[at, :] = (block * factor).astype(BF16)
        return carry

    for j in range(groups):
        mark_copies[j].wait()
        lax.fori_loop(
            j * part // mark_tile, (j + 1) * part // mark_tile, unit_marks, 0
        )

    def build(slot, first=False):
        here = pl.ds(pl.multiple_of(slot * own, own), own)

        def visit(i, carry):
            at = rows_at(i, build_tile)
            tall = jnp.exp(gamma * nt(marks_unit[at, :], unit[slot]))
            tall_b = tall.astype(BF16)
            kern_t[at, here] = tall_b
            scaled = tall * stats[0, slot, 0:1, 0:own]
            fold = scaled[:, 0:128]
            for piece in range(1, own // 128):
                fold = fold + scaled[:, piece * 128 : (piece + 1) * 128]
            product = nn(tall_b, weighted[0, here, :])
            if first:
                means[at, :] = fold
                side[at, :] = product
            else:
                means[at, :] += fold
                side[at, :] += product
            return carry

        lax.fori_loop(0, marks // build_tile, visit, 0)

    build_tile = tile(marks, BUILD)
    build(0, True)
    await_chunk(0, line)
    build(line)
    for t in range(line - 1):
        slot = relay(t)
        build(slot)
        for ref, sem in chunk_at(line + slot):
            arrived(ref, sem.at[0, line + slot])
        build(line + slot)

    weight_sum = jnp.zeros((1, 1), F32)
    for slot in range(members):
        weight_sum = weight_sum + jnp.sum(stats[0, slot, 0:1, 0:own], axis=1, keepdims=True)

    def average(i, carry):
        at = rows_at(i, mark_tile)
        total = jnp.sum(means[at, :], axis=1, keepdims=True) / weight_sum
        means[at, :] = jnp.broadcast_to(total, (mark_tile, 128))
        return carry

    lax.fori_loop(0, marks // mark_tile, average, 0)

    gaps = None
    mean_row = None
    image = None
    for step in range(ITERS):
        totals = stats[step, 0, 1:2, 0:vecs]
        squares = stats[step, 0, 2:3, 0:vecs]
        for slot in range(1, members):
            totals = totals + stats[step, slot, 1:2, 0:vecs]
            squares = squares + stats[step, slot, 2:3, 0:vecs]

        for j in [*range(1, groups), 0]:
            def centre(i, carry, j=j):
                at = pl.ds(pl.multiple_of(j * part + i * mark_tile, mark_tile), mark_tile)
                if step == 0:
                    product = side[at, :]
                else:
                    product = nn(kern_t[at, :], weighted[step])
                product = product - means[at, 0:1] * totals
                if j == 0:
                    side[at, :] = product
                else:
                    side_out[step, j, rows_at(i, mark_tile), :] = product.astype(BF16)
                return carry

            lax.fori_loop(0, part // mark_tile, centre, 0)
            side_stats_out[step, j] = jnp.zeros(side_stats_out.shape[2:], F32)
            if step == 0:
                side_stats_out[step, j, 0:1, 0:part] = jnp.transpose(
                    means[j * part : (j + 1) * part, :]
                )[0:1, :]
                side_stats_out[step, j, 1:2, 0:128] = jnp.broadcast_to(weight_sum, (1, 128))
            side_stats_out[step, j, 2:3, 0:vecs] = totals
            side_stats_out[step, j, 3:4, 0:vecs] = squares
            if j:
                back = groups - j
                to(
                    side_stats_out.at[step, j], side_stats.at[step, back],
                    grp_sems.at[step, 0, 1, j], grp_sems.at[step, 0, 0, back], grp=group(j),
                )
                to(
                    side_out.at[step, j], side_in.at[step, back],
                    grp_sems.at[step, 1, 1, j], grp_sems.at[step, 1, 0, back], grp=group(j),
                )
        said = [side_stats_out[step, 0]]
        for j in range(1, groups):
            arrived(side_stats.at[step, j], grp_sems.at[step, 0, 0, j])
            said.append(side_stats[step, j])
        if step == 0:
            all_weight = sum(s[1:2, 0:1] for s in said)
            mean_row = sum(s[0:1, 0:part] * (s[1:2, 0:1] / all_weight) for s in said)
            gaps = [s[0:1, 0:part] - mean_row for s in said]
            factor = None
        else:
            factor = 1.0 / jnp.sqrt(sum(s[3:4, 0:vecs] for s in said) / total_rows + 1e-06)
        pad = -groups % 8
        left = gaps + [jnp.zeros_like(gaps[0])] * pad
        right = [s[2:3, 0:vecs] for s in said]
        right = right + [jnp.zeros_like(right[0])] * pad
        correction = lax.dot_general(
            jnp.concatenate(left, axis=0), jnp.concatenate(right, axis=0),
            (((0,), (0,)), ((), ())), precision=HIGHEST, preferred_element_type=F32,
        )
        summed = side[0:part, :] + correction
        for j in range(1, groups):
            arrived(side_in.at[step, j], grp_sems.at[step, 1, 0, j])
            summed = summed + side_in[step, j].astype(F32)
        if factor is not None:
            summed = summed * factor
        rounded = summed.astype(BF16)
        side_b[step, 0] = jnp.transpose(summed).astype(BF16)
        shift = jnp.dot(
            jnp.broadcast_to(mean_row, (8, part)), rounded.astype(F32),
            precision=HIGHEST, preferred_element_type=F32,
        )
        shifts[step, 0] = shift
        for j in range(1, groups):
            back = groups - j
            to(
                shifts.at[step, 0], shifts.at[step, back],
                grp_sems.at[step, 2, 1, j], grp_sems.at[step, 2, 0, back], grp=group(j),
            )
            to(
                side_b.at[step, 0], side_b.at[step, back],
                grp_sems.at[step, 3, 1, j], grp_sems.at[step, 3, 0, back], grp=group(j),
            )
        for j in range(groups):
            if j:
                arrived(shifts.at[step, j], grp_sems.at[step, 2, 0, j])
                shift = shift + shifts[step, j]
                arrived(side_b.at[step, j], grp_sems.at[step, 3, 0, j])
        shift = jnp.transpose(jnp.broadcast_to(shift[0:1, :], (128, vecs)))[:, 0:1]

        def product(slot):
            whole = jnp.concatenate([side_b[step, j] for j in range(groups)], axis=1)
            return nn(whole, kern_t[:, slot * own : (slot + 1) * own]) - shift

        for k in [*order, 0]:
            image_out[step, k] = product(line + k).astype(BF16)
            to(
                image_out.at[step, k], pair_in.at[step, k],
                img_sems.at[step, 0, 1, k], img_sems.at[step, 0, 0, k], lm=mate(),
            )
        for k in order:
            mine = product(k)
            arrived(pair_in.at[step, k], img_sems.at[step, 0, 0, k])
            line_out[step, k] = (mine + pair_in[step, k].astype(F32)).astype(BF16)
            to(
                line_out.at[step, k], line_in.at[step, line - k],
                img_sems.at[step, 1, 1, k], img_sems.at[step, 1, 0, line - k], lm=along(k),
            )
        image = product(0)
        arrived(pair_in.at[step, 0], img_sems.at[step, 0, 0, 0])
        image = image + pair_in[step, 0].astype(F32)
        for k in order:
            arrived(line_in.at[step, line - k], img_sems.at[step, 1, 0, line - k])
            image = image + line_in[step, line - k].astype(F32)
        image = weight * jnp.transpose(image)
        square = jnp.sum(image * image, axis=0, keepdims=True)
        if step < ITERS - 1:
            full = weight * image
            weighted[step + 1, 0:own, :] = full.astype(BF16)
            stats[step + 1, 0, 1:2, 0:vecs] = jnp.sum(full, axis=0, keepdims=True)
            stats[step + 1, 0, 2:3, 0:vecs] = square
            spread_chunk(step + 1)
            for k in order:
                await_chunk(step + 1, line - k)
                pass_on(step + 1, line - k)
            await_chunk(step + 1, line)
            for k in order:
                await_chunk(step + 1, 2 * line - k)

    norms[0] = jnp.broadcast_to(square, norms.shape[1:])
    for k in range(1, members):
        back = members - k
        to(
            norms.at[0], norms.at[back], norm_sems.at[1, k], norm_sems.at[0, back],
            lm=(me_l + k) % members,
        )
    for k in range(1, members):
        arrived(norms.at[k], norm_sems.at[0, k])
        square = square + norms[k, 0:1, :]
    group_norms[0] = jnp.broadcast_to(square, norms.shape[1:])
    for j in range(1, groups):
        back = groups - j
        to(
            group_norms.at[0], group_norms.at[back],
            norm_sems.at[1, members + j], norm_sems.at[0, members + back], grp=group(j),
        )
    for j in range(1, groups):
        arrived(group_norms.at[j], norm_sems.at[0, members + j])
        square = square + group_norms[j, 0:1, :]
    out_ref[...] = image / jnp.sqrt(square / total_rows + 1e-06)
    for when, copy in sends:
        if when is None:
            copy.wait_send()
        else:
            pl.when(when)(copy.wait_send)


def local(groups, members, embeddings, landmarks, start_vectors, row_weight, spread):
    own, width = embeddings.shape
    marks = landmarks.shape[0]
    vecs = start_vectors.shape[1]
    rows = own * members
    part = marks // groups
    line = members // 2
    wide = max(own, vecs)
    span = max(part, vecs)
    vmem = pl.BlockSpec(memory_space=pltpu.VMEM)
    dma = pltpu.SemaphoreType.DMA
    return pl.pallas_call(
        functools.partial(kernel, groups, members),
        out_shape=jax.ShapeDtypeStruct((own, vecs), F32),
        in_specs=[pl.BlockSpec(memory_space=pltpu.SMEM), vmem, pl.BlockSpec(memory_space=pl.ANY), vmem, vmem],
        out_specs=vmem,
        scratch_shapes=[
            pltpu.VMEM((marks, width), BF16),
            pltpu.VMEM((marks, width), BF16),
            pltpu.VMEM((marks, rows), BF16),
            pltpu.VMEM((members, own, width), BF16),
            pltpu.VMEM((ITERS, rows, vecs), BF16),
            pltpu.VMEM((ITERS, members, 8, wide), F32),
            pltpu.VMEM((marks, vecs), F32),
            pltpu.VMEM((marks, 128), F32),
            pltpu.VMEM((ITERS, groups, part, vecs), BF16),
            pltpu.VMEM((ITERS, groups, part, vecs), BF16),
            pltpu.VMEM((ITERS, groups, 8, span), F32),
            pltpu.VMEM((ITERS, groups, 8, span), F32),
            pltpu.VMEM((ITERS, groups, vecs, part), BF16),
            pltpu.VMEM((ITERS, groups, 8, vecs), F32),
            pltpu.VMEM((ITERS, line, vecs, own), BF16),
            pltpu.VMEM((ITERS, line, vecs, own), BF16),
            pltpu.VMEM((ITERS, line, vecs, own), BF16),
            pltpu.VMEM((ITERS, line, vecs, own), BF16),
            pltpu.VMEM((members, 8, vecs), F32),
            pltpu.VMEM((groups, 8, vecs), F32),
            dma((ITERS, 4, 3, members)),
            dma((1,)),
            dma((ITERS, 4, 2, groups)),
            dma((ITERS, 2, 2, line)),
            dma((2, members + groups)),
            dma((groups,)),
        ],
        compiler_params=pltpu.CompilerParams(
            collective_id=0, has_side_effects=True, vmem_limit_bytes=62 * 2**20
        ),
    )(spread, embeddings, landmarks, start_vectors, row_weight.reshape(1, own))


def solution(mesh):
    groups, members = mesh.shape["grp"], mesh.shape["lm"]
    in_specs = (
        P(("grp", "lm"), None),
        P("lm", None),
        P(("grp", "lm"), None),
        P(("grp", "lm")),
        P(),
    )
    return jax.shard_map(
        functools.partial(local, groups, members), mesh=mesh, in_specs=in_specs,
        out_specs=P(("grp", "lm"), None), check_vma=False,
    )
```

profile of v0, /device:TPU:0, one launch (start us, length us, event | category | flops | bytes accessed | tf_op | source)
XLA Modules:
  0.0 110.5 jit_solution(2437979209754179243)
XLA Ops:
  0.7 108.3 %shard_map.55 = f32[256,128]{1,0:T(8,128)} custom-call(f32[1]{0:T(128)S(6)} %copy.7.spread_ref, bf16[256,512]{1,0:T(8,128)(2,1)} %emb_ref.1, bf16[2048,512]{1,0:T(8,128)(2,1)} %marks_ref.1, f32[256,128]{1,0:T(8,128)} %vec_ref.1, f32[1,256]{1,0:T(1,128)} %bitcast.1), custom_call_target="tpu_custom_call" | custom-call | tf_op jit(solution)/shard_map/pallas_call | solution.py:422
  109.0 1.6 %copy.8 = f32[256,128]{1,0:T(8,128)} copy(f32[256,128]{1,0:T(8,128)} %shard_map.55) | data formatting | bytes 262144
where the time goes:
time: 111 us
  Pallas kernels  108 us (97%)
  local copies, waits for them, and re-layouts  1.57 us (1%)
    pallas_call x1, Pallas kernels, local(): pl.pallas_call(functools.partial(kernel, groups, members), out_shape=jax....  108 us

commit v1 on v0

v1 whole, which is shorter than its diff:
```python
import functools

import jax
import jax.numpy as jnp
from jax import lax
from jax.experimental import pallas as pl
from jax.experimental.pallas import tpu as pltpu
from jax.sharding import PartitionSpec as P

ITERS = 2
HALVES = 2
F32 = jnp.float32
BF16 = jnp.bfloat16
BUILD = 1024
HIGHEST = lax.Precision.HIGHEST


def nt(a, b):
    return lax.dot_general(a, b, (((1,), (1,)), ((), ())), preferred_element_type=F32)


def nn(a, b):
    return jnp.dot(a, b, preferred_element_type=F32)


def tile(total, most):
    size = min(total, most)
    while total % size:
        size -= 8
    return size


def rows_at(index, size):
    return pl.ds(pl.multiple_of(index * size, size), size)


def column(row):
    return jnp.transpose(jnp.broadcast_to(row, (128, row.shape[1])))[:, 0:1]


def visits(z, line):
    left, right = z, line - 1 - z
    found = []
    for ahead, behind, from_left in ((left, right, True), (right, left, False)):
        for d in range(1, ahead + 1):
            if d == 1:
                key = 1 if ahead <= behind else 2
            elif d == 2:
                key = 0 if behind else 3
            else:
                key = d + 1
            found.append((key, d, from_left))
    return [(d, from_left) for _, d, from_left in sorted(found)]


def kernel(
    groups, members, spread_ref, emb_ref, marks_ref, vec_ref, weight_ref, out_ref,
    marks_in, marks_unit, kern_t, unit, wt, first_stats, stats, side, means, mean_rows,
    mean_all, side_out, side_in, side_acc, lead_out, lead_in, follow_out, follow_in,
    side_b, image_out, pair_in, line_out, line_in, held, norms, group_norms,
    row_sems, wt_sems, lead_sems, grp_sems, img_sems, norm_sems, mark_sems,
):
    own, width = emb_ref.shape
    marks = marks_ref.shape[0]
    vecs = vec_ref.shape[1]
    part = marks // groups
    line = members // 2
    total_rows = own * groups * members
    hv = vecs // HALVES
    me_g = lax.axis_index("grp")
    me_l = lax.axis_index("lm")
    z = me_l // 2
    c = me_l % 2
    sends = []
    half = own // 2

    def to(src, dst, send_sem, recv_sem, when=None, **device):
        copy = pltpu.make_async_remote_copy(
            src_ref=src, dst_ref=dst, send_sem=send_sem, recv_sem=recv_sem,
            device_id=device, device_id_type=pl.DeviceIdType.MESH,
        )
        if when is None:
            copy.start()
        else:
            pl.when(when)(copy.start)
        sends.append((when, copy))

    def arrived(ref, sem):
        pltpu.make_async_remote_copy(
            src_ref=ref, dst_ref=ref, send_sem=sem, recv_sem=sem,
            device_id={"lm": me_l}, device_id_type=pl.DeviceIdType.MESH,
        ).wait_recv()

    def mate():
        return z * 2 + 1 - c

    def along(k):
        return (z + k) % line * 2 + c

    def group(j):
        return (me_g + j) % groups

    order = sorted(range(1, line), key=lambda k: min(k, line - k))

    barrier = pltpu.get_barrier_semaphore()
    for k in range(1, members):
        pl.semaphore_signal(
            barrier, inc=1, device_id={"lm": (me_l + k) % members},
            device_id_type=pl.DeviceIdType.MESH,
        )
    for j in range(1, groups):
        pl.semaphore_signal(
            barrier, inc=1, device_id={"grp": group(j)}, device_id_type=pl.DeviceIdType.MESH
        )

    mark_copies = []
    for j in range(groups):
        mark_copies.append(pltpu.make_async_copy(
            marks_ref.at[pl.ds(pl.multiple_of(group(j) * part, part), part), :],
            marks_in.at[pl.ds(j * part, part), :], mark_sems.at[j],
        ))
        mark_copies[j].start()

    gamma = spread_ref[0]
    weight_row = weight_ref[...]
    values = emb_ref[...].astype(F32)
    scale = lax.rsqrt(jnp.sum(values * values, axis=1, keepdims=True) + 1e-06)
    unit[0] = (values * scale).astype(BF16)

    def stat_rows(columns):
        lane = lax.broadcasted_iota(jnp.int32, (columns[0].shape[0], 128), 1)
        wide = jnp.zeros(lane.shape, F32)
        for i, col in enumerate(columns):
            wide = jnp.where(lane == i, col, wide)
        return jnp.transpose(wide)[0:8, :]

    full = weight_row * jnp.transpose(vec_ref[...])
    first_stats[0] = jnp.zeros(first_stats.shape[1:], F32)
    first_stats[0, 0:1, 0:own] = weight_row
    for h in range(HALVES):
        piece = full[h * hv : (h + 1) * hv, :]
        wt[0, 0, h] = piece.astype(BF16)
        first_stats[0, 1 + h : 2 + h, 0:hv] = stat_rows(
            [jnp.sum(piece, axis=1, keepdims=True)]
        )[0:1, :]
    pl.semaphore_wait(barrier, members - 1 + groups - 1)

    def chunk(slot):
        return [
            (unit.at[slot, pl.ds(0, half), :], row_sems.at[0]),
            (unit.at[slot, pl.ds(half, half), :], row_sems.at[1]),
            (wt.at[0, slot], row_sems.at[2]),
            (first_stats.at[slot], row_sems.at[3]),
        ]

    for (src, sem), (dst, _) in zip(chunk(0), chunk(line)):
        to(src, dst, sem.at[2, 0], sem.at[0, line], lm=mate())
    for d in (2, 1):
        if d < line:
            for right in (1, 0):
                slot = line - d if right else d
                for (src, sem), (dst, _) in zip(chunk(0), chunk(slot)):
                    to(
                        src, dst, sem.at[1, line + 2 * (d - 1) + right], sem.at[0, slot],
                        when=z < line - d if right else z >= d,
                        lm=(z + d if right else z + line - d) % line * 2 + c,
                    )

    mark_tile = tile(part, 256)

    def unit_marks(i, carry):
        at = rows_at(i, mark_tile)
        block = marks_in[at, :].astype(F32)
        factor = lax.rsqrt(jnp.sum(block * block, axis=1, keepdims=True) + 1e-06)
        marks_unit[at, :] = (block * factor).astype(BF16)
        return carry

    for j in range(groups):
        mark_copies[j].wait()
        lax.fori_loop(
            j * part // mark_tile, (j + 1) * part // mark_tile, unit_marks, 0
        )

    def at_z(table):
        found = jnp.int32(table[0])
        for position in range(1, line):
            found = jnp.where(z == position, jnp.int32(table[position]), found)
        return found

    def relay(t):
        plan = [visits(position, line)[t] for position in range(line)]
        slot = at_z([line - d if left else d for d, left in plan])
        left = at_z([int(left) for _, left in plan]) == 1
        more = at_z([
            int(d >= 2 and (position < line - 1 if left else position > 0))
            for position, (d, left) in enumerate(plan)
        ]) == 1
        follow = jnp.where(more, jnp.where(left, slot - 1, slot + 1), slot)
        for (src, sem), (dst, _) in zip(chunk(slot), chunk(follow)):
            arrived(src, sem.at[0, slot])
            to(
                src, dst, sem.at[1, slot], sem.at[0, follow], when=more,
                lm=jnp.where(left, z + 1, z - 1 + line) % line * 2 + c,
            )
        for (src, sem), (dst, _) in zip(chunk(slot), chunk(line + slot)):
            to(src, dst, sem.at[2, slot], sem.at[0, line + slot], lm=mate())
        return slot

    def build(slot, first=False):
        here = pl.ds(pl.multiple_of(slot * own, own), own)

        def visit(i, carry):
            at = rows_at(i, build_tile)
            tall = jnp.exp(gamma * nt(marks_unit[at, :], unit[slot]))
            tall_b = tall.astype(BF16)
            kern_t[at, here] = tall_b
            scaled = tall * first_stats[slot, 0:1, 0:own]
            fold = scaled[:, 0:128]
            for piece in range(1, own // 128):
                fold = fold + scaled[:, piece * 128 : (piece + 1) * 128]
            product = nt(tall_b, wt[0, slot].reshape(vecs, own))
            if first:
                means[at, :] = fold
                side[at, :] = product
            else:
                means[at, :] += fold
                side[at, :] += product
            return carry

        lax.fori_loop(0, marks // build_tile, visit, 0)

    build_tile = tile(marks, BUILD)
    build(0, True)
    for ref, sem in chunk(line):
        arrived(ref, sem.at[0, line])
    build(line)
    for t in range(line - 1):
        slot = relay(t)
        build(slot)
        for ref, sem in chunk(line + slot):
            arrived(ref, sem.at[0, line + slot])
        build(line + slot)

    def parts():
        return [*range(1, groups), 0]

    def send_side(step, h, j):
        to(
            side_out.at[step, h, j], side_in.at[step, h, groups - j],
            grp_sems.at[step, h, 0, 1, j], grp_sems.at[step, h, 0, 0, groups - j],
            grp=group(j),
        )

    def first_side():
        weight_sum = jnp.zeros((1, 1), F32)
        rows = jnp.zeros((8, 128), F32)
        for slot in range(members):
            weight_sum = weight_sum + jnp.sum(
                first_stats[slot, 0:1, 0:own], axis=1, keepdims=True
            )
            rows = rows + first_stats[slot, :, 0:128]
        totals = [column(rows[1 + h : 2 + h, 0:128])[0:hv] for h in range(HALVES)]
        totals = jnp.concatenate(totals, axis=0)
        for j in parts():
            span = pl.ds(j * part, part)
            mean = jnp.sum(jnp.transpose(means[span, :]), axis=0, keepdims=True) / weight_sum
            mean_rows[j] = jnp.broadcast_to(mean, (8, part))
            block = jnp.transpose(side[span, :]) - totals * mean
            lead_out[j] = jnp.zeros(lead_out.shape[1:], F32)
            lead_out[j, 0:1, 0:part] = mean
            lead_out[j, 1:2, 0:128] = jnp.broadcast_to(weight_sum, (1, 128))
            lead_out[j, 2 : 2 + HALVES, 0:128] = rows[1 : 1 + HALVES, :]
            if j:
                to(
                    lead_out.at[j], lead_in.at[groups - j],
                    lead_sems.at[0, 1, j], lead_sems.at[0, 0, groups - j], grp=group(j),
                )
            for h in range(HALVES):
                piece = block[h * hv : (h + 1) * hv, :]
                if j:
                    side_out[0, h, j] = piece.astype(BF16)
                    if h == 0:
                        send_side(0, h, j)
                else:
                    side_acc[h, 0] = piece
        for h in range(1, HALVES):
            for j in range(1, groups):
                send_side(0, h, j)

    def line_chunk(step, h, slot):
        return [
            (wt.at[step, slot, h], wt_sems.at[step - 1, h, 0]),
            (stats.at[step - 1, h, slot], wt_sems.at[step - 1, h, 1]),
        ]

    def next_side(step, h):
        for k in order:
            back = line - k
            for (src, sem), (dst, _) in zip(
                line_chunk(step, h, back), line_chunk(step, h, line + back)
            ):
                arrived(src, sem.at[0, back])
                to(src, dst, sem.at[1, line + back], sem.at[0, line + back], lm=mate())

        def product(j, low):
            vectors = [wt[step, slot, h] for slot in range(low, low + line)]
            return nt(
                jnp.concatenate(vectors, axis=1),
                kern_t[j * part : (j + 1) * part, low * own : (low + line) * own],
            )

        for j in parts():
            side_acc[h, j] = product(j, 0)
        for slot in range(line, members):
            for ref, sem in line_chunk(step, h, slot):
                arrived(ref, sem.at[0, slot])
        rows = stats[step - 1, h, 0]
        for slot in range(1, members):
            rows = rows + stats[step - 1, h, slot]
        follow_out[step - 1, h] = rows
        for j in range(1, groups):
            to(
                follow_out.at[step - 1, h], follow_in.at[step - 1, h, groups - j],
                grp_sems.at[step, h, 2, 1, j], grp_sems.at[step, h, 2, 0, groups - j],
                grp=group(j),
            )
        totals = column(rows[0:1, :])[0:hv]
        for j in parts():
            block = side_acc[h, j] + product(j, line) - totals * mean_rows[j, 0:1, :]
            if j:
                side_out[step, h, j] = block.astype(BF16)
                send_side(step, h, j)
            else:
                side_acc[h, 0] = block

    def flat(rows, height):
        pad = -height % 8
        return jnp.concatenate(rows + [jnp.zeros_like(rows[0])] * pad, axis=0)

    def gather_side(step, h, shared):
        if step == 0 and h == 0:
            said = [lead_out[0]]
            for j in range(1, groups):
                arrived(lead_in.at[j], lead_sems.at[0, 0, j])
                said.append(lead_in[j])
            all_weight = sum(s[1:2, 0:1] for s in said)
            mean_row = sum(s[0:1, 0:part] * (s[1:2, 0:1] / all_weight) for s in said)
            mean_all[0] = jnp.broadcast_to(mean_row, (8, part))
            for j in range(1, groups):
                to(
                    mean_all.at[0], mean_all.at[groups - j],
                    lead_sems.at[1, 1, j], lead_sems.at[1, 0, groups - j], grp=group(j),
                )
            shared["gaps"] = flat([s[0:1, 0:part] - mean_row for s in said], groups)
            shared["totals"] = [
                [s[2 + i : 3 + i, 0:128] for s in said] for i in range(HALVES)
            ]
        factor = None
        if step == 0:
            totals = shared["totals"][h]
        else:
            said = [follow_out[step - 1, h]]
            for j in range(1, groups):
                arrived(follow_in.at[step - 1, h, j], grp_sems.at[step, h, 2, 0, j])
                said.append(follow_in[step - 1, h, j])
            totals = [s[0:1, :] for s in said]
            factor = column(
                1.0 / jnp.sqrt(sum(s[1:2, :] for s in said) / total_rows + 1e-06)
            )[0:hv]
        correction = lax.dot_general(
            flat(totals, groups), shared["gaps"],
            (((0,), (0,)), ((), ())), precision=HIGHEST, preferred_element_type=F32,
        )[0:hv]
        summed = side_acc[h, 0] + correction
        for j in range(1, groups):
            arrived(side_in.at[step, h, j], grp_sems.at[step, h, 0, 0, j])
            summed = summed + side_in[step, h, j].astype(F32)
        if factor is not None:
            summed = summed * factor
        side_b[step, h, 0] = summed.astype(BF16)
        for j in range(1, groups):
            to(
                side_b.at[step, h, 0], side_b.at[step, h, groups - j],
                grp_sems.at[step, h, 1, 1, j], grp_sems.at[step, h, 1, 0, groups - j],
                grp=group(j),
            )

    wide = 2 if line % 2 == 0 else 1

    def make_image(step, h):
        if step == 0 and h == 0:
            for j in range(1, groups):
                arrived(mean_all.at[j], lead_sems.at[1, 0, j])
        weighed = jnp.zeros((hv, part), F32)
        blocks = []
        for j in range(groups):
            if j:
                arrived(side_b.at[step, h, j], grp_sems.at[step, h, 1, 0, j])
            blocks.append(side_b[step, h, j])
            weighed = weighed + blocks[j].astype(F32) * mean_all[j, 0:1, :]
        shift = jnp.sum(weighed, axis=1, keepdims=True)
        whole = jnp.concatenate(blocks, axis=1)

        def product(slot):
            result = nn(whole, kern_t[:, slot * own : (slot + wide) * own]) - shift
            return [result[:, i * own : (i + 1) * own] for i in range(wide)]

        starts = range(line - wide, -1, -wide)
        for start in starts:
            pieces = product(line + start)
            for i in reversed(range(wide)):
                k = start + i
                image_out[step, h, k] = pieces[i].astype(BF16)
                to(
                    image_out.at[step, h, k], pair_in.at[step, h, k],
                    img_sems.at[step, h, 0, 1, k], img_sems.at[step, h, 0, 0, k], lm=mate(),
                )
        for start in starts:
            pieces = product(start)
            for i in reversed(range(wide)):
                k = start + i
                arrived(pair_in.at[step, h, k], img_sems.at[step, h, 0, 0, k])
                mine = pieces[i] + pair_in[step, h, k].astype(F32)
                if k == 0:
                    held[h] = mine
                    continue
                line_out[step, h, k] = mine.astype(BF16)
                to(
                    line_out.at[step, h, k], line_in.at[step, h, line - k],
                    img_sems.at[step, h, 1, 1, k], img_sems.at[step, h, 1, 0, line - k],
                    lm=along(k),
                )

    def end_image(step, h):
        image = held[h]
        for k in order:
            arrived(line_in.at[step, h, line - k], img_sems.at[step, h, 1, 0, line - k])
            image = image + line_in[step, h, line - k].astype(F32)
        image = weight_row * image
        square = jnp.sum(image * image, axis=1, keepdims=True)
        if step == ITERS - 1:
            held[h] = image
            return square
        full = weight_row * image
        wt[step + 1, 0, h] = full.astype(BF16)
        rows = stat_rows([jnp.sum(full, axis=1, keepdims=True), square])
        stats[step, h, 0] = jnp.zeros((8, 128), F32)
        stats[step, h, 0, :, 0:hv] = rows
        own_chunk = line_chunk(step + 1, h, 0)
        for (src, sem), (dst, _) in zip(own_chunk, line_chunk(step + 1, h, line)):
            to(src, dst, sem.at[1, 0], sem.at[0, line], lm=mate())
        for k in order:
            for (src, sem), (dst, _) in zip(own_chunk, line_chunk(step + 1, h, line - k)):
                to(src, dst, sem.at[1, k], sem.at[0, line - k], lm=along(k))
        return square

    shared = {}
    squares = []
    for step in range(ITERS):
        if step == 0:
            first_side()
        else:
            for h in range(HALVES):
                next_side(step, h)
        for h in range(HALVES):
            gather_side(step, h, shared)
        for h in range(HALVES):
            make_image(step, h)
        squares = [end_image(step, h) for h in range(HALVES)]

    square = stat_rows([jnp.concatenate(squares, axis=0)])[0:1, :]
    norms[0] = jnp.broadcast_to(square, norms.shape[1:])
    for k in range(1, members):
        back = members - k
        to(
            norms.at[0], norms.at[back], norm_sems.at[1, k], norm_sems.at[0, back],
            lm=(me_l + k) % members,
        )
    for k in range(1, members):
        arrived(norms.at[k], norm_sems.at[0, k])
        square = square + norms[k, 0:1, :]
    group_norms[0] = jnp.broadcast_to(square, norms.shape[1:])
    for j in range(1, groups):
        back = groups - j
        to(
            group_norms.at[0], group_norms.at[back],
            norm_sems.at[1, members + j], norm_sems.at[0, members + back], grp=group(j),
        )
    for j in range(1, groups):
        arrived(group_norms.at[j], norm_sems.at[0, members + j])
        square = square + group_norms[j, 0:1, :]
    image = jnp.transpose(jnp.concatenate([held[h] for h in range(HALVES)], axis=0))
    out_ref[...] = image / jnp.sqrt(square / total_rows + 1e-06)
    for when, copy in sends:
        if when is None:
            copy.wait_send()
        else:
            pl.when(when)(copy.wait_send)


def local(groups, members, embeddings, landmarks, start_vectors, row_weight, spread):
    own, width = embeddings.shape
    marks = landmarks.shape[0]
    vecs = start_vectors.shape[1]
    rows = own * members
    part = marks // groups
    line = members // 2
    hv = vecs // HALVES
    wide = max(own, 128)
    span = max(part, 128)
    vmem = pl.BlockSpec(memory_space=pltpu.VMEM)
    dma = pltpu.SemaphoreType.DMA
    return pl.pallas_call(
        functools.partial(kernel, groups, members),
        out_shape=jax.ShapeDtypeStruct((own, vecs), F32),
        in_specs=[pl.BlockSpec(memory_space=pltpu.SMEM), vmem, pl.BlockSpec(memory_space=pl.ANY), vmem, vmem],
        out_specs=vmem,
        scratch_shapes=[
            pltpu.VMEM((marks, width), BF16),
            pltpu.VMEM((marks, width), BF16),
            pltpu.VMEM((marks, rows), BF16),
            pltpu.VMEM((members, own, width), BF16),
            pltpu.VMEM((ITERS, members, HALVES, hv, own), BF16),
            pltpu.VMEM((members, 8, wide), F32),
            pltpu.VMEM((ITERS - 1, HALVES, members, 8, 128), F32),
            pltpu.VMEM((marks, vecs), F32),
            pltpu.VMEM((marks, 128), F32),
            pltpu.VMEM((groups, 8, part), F32),
            pltpu.VMEM((groups, 8, part), F32),
            pltpu.VMEM((ITERS, HALVES, groups, hv, part), BF16),
            pltpu.VMEM((ITERS, HALVES, groups, hv, part), BF16),
            pltpu.VMEM((HALVES, groups, hv, part), F32),
            pltpu.VMEM((groups, 8, span), F32),
            pltpu.VMEM((groups, 8, span), F32),
            pltpu.VMEM((ITERS - 1, HALVES, 8, 128), F32),
            pltpu.VMEM((ITERS - 1, HALVES, groups, 8, 128), F32),
            pltpu.VMEM((ITERS, HALVES, groups, hv, part), BF16),
            pltpu.VMEM((ITERS, HALVES, line, hv, own), BF16),
            pltpu.VMEM((ITERS, HALVES, line, hv, own), BF16),
            pltpu.VMEM((ITERS, HALVES, line, hv, own), BF16),
            pltpu.VMEM((ITERS, HALVES, line, hv, own), BF16),
            pltpu.VMEM((HALVES, hv, own), F32),
            pltpu.VMEM((members, 8, vecs), F32),
            pltpu.VMEM((groups, 8, vecs), F32),
            dma((4, 3, members + 4)),
            dma((ITERS - 1, HALVES, 2, 2, members)),
            dma((2, 2, groups)),
            dma((ITERS, HALVES, 3, 2, groups)),
            dma((ITERS, HALVES, 2, 2, line)),
            dma((2, members + groups)),
            dma((groups,)),
        ],
        compiler_params=pltpu.CompilerParams(
            collective_id=0, has_side_effects=True, vmem_limit_bytes=62 * 2**20
        ),
    )(spread, embeddings, landmarks, start_vectors, row_weight.reshape(1, own))


def solution(mesh):
    groups, members = mesh.shape["grp"], mesh.shape["lm"]
    in_specs = (
        P(("grp", "lm"), None),
        P("lm", None),
        P(("grp", "lm"), None),
        P(("grp", "lm")),
        P(),
    )
    return jax.shard_map(
        functools.partial(local, groups, members), mesh=mesh, in_specs=in_specs,
        out_specs=P(("grp", "lm"), None), check_vma=False,
    )
```

time: 111 us -> 96.1 us (0.87)
  Pallas kernels: 108 us -> 93.7 us
    pallas_call x1, Pallas kernels: 108 us -> 93.7 us  [local(): pl.pallas_call(functools.partial(kernel, groups, members), out_shape=jax....]
where the time goes in v1:
time: 96.1 us; the launch traced here: 95.9 us
  Pallas kernels  93.7 us (98%)
  local copies, waits for them, and re-layouts  1.57 us (2%)
    pallas_call x1, Pallas kernels, local(): pl.pallas_call(functools.partial(kernel, groups, members), out_shape=jax....  93.7 us

profile of v1, /device:TPU:0, one launch (start us, length us, event | category | flops | bytes accessed | tf_op | source)
XLA Modules:
  0.0 95.9 jit_solution(1060683351979986662)
XLA Ops:
  0.7 93.7 %shard_map.55 = f32[256,128]{1,0:T(8,128)} custom-call(f32[1]{0:T(128)S(6)} %copy.7.spread_ref, bf16[256,512]{1,0:T(8,128)(2,1)} %emb_ref.1, bf16[2048,512]{1,0:T(8,128)(2,1)} %marks_ref.1, f32[256,128]{1,0:T(8,128)} %vec_ref.1, f32[1,256]{1,0:T(1,128)} %bitcast.1), custom_call_target="tpu_custom_call" | custom-call | tf_op jit(solution)/shard_map/pallas_call | solution.py:513
  94.4 1.6 %copy.8 = f32[256,128]{1,0:T(8,128)} copy(f32[256,128]{1,0:T(8,128)} %shard_map.55) | data formatting | bytes 262144

commit v2 on v1

--- a/solution.py
+++ b/solution.py
@@ -1,4 +1,5 @@
 import functools
+import math
 
 import jax
 import jax.numpy as jnp
@@ -54,11 +55,12 @@
 
 
 def kernel(
-    groups, members, spread_ref, emb_ref, marks_ref, vec_ref, weight_ref, out_ref,
-    marks_in, marks_unit, kern_t, unit, wt, first_stats, stats, side, means, mean_rows,
+    groups, members, spread_hbm, emb_hbm, marks_ref, vec_hbm, weight_hbm, out_ref,
+    spread_ref, emb_ref, vec_ref, weight_ref, marks_in, marks_unit, kern_t, unit, wt, first_stats, stats, side, means, mean_rows,
     mean_all, side_out, side_in, side_acc, lead_out, lead_in, follow_out, follow_in,
     side_b, image_out, pair_in, line_out, line_in, held, norms, group_norms,
-    row_sems, wt_sems, lead_sems, grp_sems, img_sems, norm_sems, mark_sems,
+    row_sems, own_sems, wt_sems, lead_sems, grp_sems, img_sems, norm_sems, sent_sems,
+    mark_sems, in_sems,
 ):
     own, width = emb_ref.shape
     marks = marks_ref.shape[0]
@@ -71,25 +73,43 @@
     me_l = lax.axis_index("lm")
     z = me_l // 2
     c = me_l % 2
-    sends = []
     half = own // 2
+    sends = {}
+
+    def size(ref):
+        return math.prod(ref.shape) * jnp.dtype(ref.dtype).itemsize
 
     def to(src, dst, send_sem, recv_sem, when=None, **device):
+        name, sem = send_sem
         copy = pltpu.make_async_remote_copy(
-            src_ref=src, dst_ref=dst, send_sem=send_sem, recv_sem=recv_sem,
+            src_ref=src, dst_ref=dst, send_sem=sem, recv_sem=recv_sem,
             device_id=device, device_id_type=pl.DeviceIdType.MESH,
         )
         if when is None:
             copy.start()
         else:
             pl.when(when)(copy.start)
-        sends.append((when, copy))
-
-    def arrived(ref, sem):
-        pltpu.make_async_remote_copy(
+        _, _, total = sends.get(name, (None, None, 0))
+        sends[name] = (when, sem, total + size(src))
+
+    def bytes_of(total):
+        unit = 16 * 128 * 2
+        blocks = total // unit
+        across = 1
+        while blocks % across or blocks // across > marks // 16:
+            across += 1
+        return kern_t.at[pl.ds(0, blocks // across * 16), pl.ds(0, across * 128)]
+
+    def waiter(ref, sem):
+        return pltpu.make_async_remote_copy(
             src_ref=ref, dst_ref=ref, send_sem=sem, recv_sem=sem,
             device_id={"lm": me_l}, device_id_type=pl.DeviceIdType.MESH,
-        ).wait_recv()
+        )
+
+    def arrived(refs, sem):
+        refs = refs if isinstance(refs, list) else [refs]
+        ref = refs[0] if len(refs) == 1 else bytes_of(sum(map(size, refs)))
+        waiter(ref, sem).wait_recv()
 
     def mate():
         return z * 2 + 1 - c
@@ -113,6 +133,13 @@
             barrier, inc=1, device_id={"grp": group(j)}, device_id_type=pl.DeviceIdType.MESH
         )
 
+    inputs = []
+    for i, (src, dst) in enumerate((
+        (emb_hbm, emb_ref), (weight_hbm, weight_ref), (vec_hbm, vec_ref),
+        (spread_hbm, spread_ref),
+    )):
+        inputs.append(pltpu.make_async_copy(src, dst, in_sems.at[i]))
+        inputs[i].start()
     mark_copies = []
     for j in range(groups):
         mark_copies.append(pltpu.make_async_copy(
@@ -121,8 +148,7 @@
         ))
         mark_copies[j].start()
 
-    gamma = spread_ref[0]
-    weight_row = weight_ref[...]
+    inputs[0].wait()
     values = emb_ref[...].astype(F32)
     scale = lax.rsqrt(jnp.sum(values * values, axis=1, keepdims=True) + 1e-06)
     unit[0] = (values * scale).astype(BF16)
@@ -134,6 +160,41 @@
             wide = jnp.where(lane == i, col, wide)
         return jnp.transpose(wide)[0:8, :]
 
+    pl.semaphore_wait(barrier, members - 1 + groups - 1)
+
+    def chunk(slot):
+        return [
+            ([unit.at[slot, pl.ds(0, half), :]], row_sems.at[0]),
+            ([unit.at[slot, pl.ds(half, half), :]], row_sems.at[1]),
+            ([wt.at[0, slot], first_stats.at[slot]], row_sems.at[2]),
+        ]
+
+    def send(sources, targets, name, sem, slot, when=None, **device):
+        for (srcs, _), (dsts, recv) in zip(sources, targets):
+            for src, dst in zip(srcs, dsts):
+                to(src, dst, (name, sem), recv.at[slot], when, **device)
+
+    def send_own(low, high):
+        def pieces(slot):
+            return chunk(slot)[low:high]
+
+        send(pieces(0), pieces(line), "mate", own_sems.at[0], line, lm=mate())
+        for d in (2, 1):
+            if d < line:
+                for right in (1, 0):
+                    slot = line - d if right else d
+                    send(
+                        pieces(0), pieces(slot), f"own {d} {right}",
+                        own_sems.at[2 * d + right - 1], slot,
+                        when=z < line - d if right else z >= d,
+                        lm=(z + d if right else z + line - d) % line * 2 + c,
+                    )
+
+    send_own(0, 2)
+    for copy in inputs[1:]:
+        copy.wait()
+    gamma = spread_ref[0]
+    weight_row = weight_ref[...]
     full = weight_row * jnp.transpose(vec_ref[...])
     first_stats[0] = jnp.zeros(first_stats.shape[1:], F32)
     first_stats[0, 0:1, 0:own] = weight_row
@@ -143,28 +204,7 @@
         first_stats[0, 1 + h : 2 + h, 0:hv] = stat_rows(
             [jnp.sum(piece, axis=1, keepdims=True)]
         )[0:1, :]
-    pl.semaphore_wait(barrier, members - 1 + groups - 1)
-
-    def chunk(slot):
-        return [
-            (unit.at[slot, pl.ds(0, half), :], row_sems.at[0]),
-            (unit.at[slot, pl.ds(half, half), :], row_sems.at[1]),
-            (wt.at[0, slot], row_sems.at[2]),
-            (first_stats.at[slot], row_sems.at[3]),
-        ]
-
-    for (src, sem), (dst, _) in zip(chunk(0), chunk(line)):
-        to(src, dst, sem.at[2, 0], sem.at[0, line], lm=mate())
-    for d in (2, 1):
-        if d < line:
-            for right in (1, 0):
-                slot = line - d if right else d
-                for (src, sem), (dst, _) in zip(chunk(0), chunk(slot)):
-                    to(
-                        src, dst, sem.at[1, line + 2 * (d - 1) + right], sem.at[0, slot],
-                        when=z < line - d if right else z >= d,
-                        lm=(z + d if right else z + line - d) % line * 2 + c,
-                    )
+    send_own(2, 3)
 
     mark_tile = tile(part, 256)
 
@@ -196,14 +236,13 @@
             for position, (d, left) in enumerate(plan)
         ]) == 1
         follow = jnp.where(more, jnp.where(left, slot - 1, slot + 1), slot)
-        for (src, sem), (dst, _) in zip(chunk(slot), chunk(follow)):
-            arrived(src, sem.at[0, slot])
-            to(
-                src, dst, sem.at[1, slot], sem.at[0, follow], when=more,
+        for source, target in zip(chunk(slot), chunk(follow)):
+            arrived(source[0], source[1].at[slot])
+            send(
+                [source], [target], f"relay {t}", own_sems.at[5 + t], follow, when=more,
                 lm=jnp.where(left, z + 1, z - 1 + line) % line * 2 + c,
             )
-        for (src, sem), (dst, _) in zip(chunk(slot), chunk(line + slot)):
-            to(src, dst, sem.at[2, slot], sem.at[0, line + slot], lm=mate())
+        send(chunk(slot), chunk(line + slot), "mate", own_sems.at[0], line + slot, lm=mate())
         return slot
 
     def build(slot, first=False):
@@ -231,14 +270,16 @@
 
     build_tile = tile(marks, BUILD)
     build(0, True)
-    for ref, sem in chunk(line):
-        arrived(ref, sem.at[0, line])
+    def await_mate(slot):
+        for refs, sem in chunk(slot):
+            arrived(refs, sem.at[slot])
+
+    await_mate(line)
     build(line)
     for t in range(line - 1):
         slot = relay(t)
         build(slot)
-        for ref, sem in chunk(line + slot):
-            arrived(ref, sem.at[0, line + slot])
+        await_mate(line + slot)
         build(line + slot)
 
     def parts():
@@ -247,8 +288,7 @@
     def send_side(step, h, j):
         to(
             side_out.at[step, h, j], side_in.at[step, h, groups - j],
-            grp_sems.at[step, h, 0, 1, j], grp_sems.at[step, h, 0, 0, groups - j],
-            grp=group(j),
+            ("side", sent_sems.at[0]), grp_sems.at[h, 0, groups - j], grp=group(j),
         )
 
     def first_side():
@@ -273,7 +313,7 @@
             if j:
                 to(
                     lead_out.at[j], lead_in.at[groups - j],
-                    lead_sems.at[0, 1, j], lead_sems.at[0, 0, groups - j], grp=group(j),
+                    ("lead", sent_sems.at[1]), lead_sems.at[0, groups - j], grp=group(j),
                 )
             for h in range(HALVES):
                 piece = block[h * hv : (h + 1) * hv, :]
@@ -288,19 +328,17 @@
                 send_side(0, h, j)
 
     def line_chunk(step, h, slot):
-        return [
-            (wt.at[step, slot, h], wt_sems.at[step - 1, h, 0]),
-            (stats.at[step - 1, h, slot], wt_sems.at[step - 1, h, 1]),
-        ]
+        return [wt.at[step, slot, h], stats.at[step - 1, h, slot]]
+
+    def send_line(step, h, source, target, **device):
+        for src, dst in zip(line_chunk(step, h, source), line_chunk(step, h, target)):
+            to(src, dst, ("line", sent_sems.at[2]), wt_sems.at[h, target], **device)
 
     def next_side(step, h):
         for k in order:
             back = line - k
-            for (src, sem), (dst, _) in zip(
-                line_chunk(step, h, back), line_chunk(step, h, line + back)
-            ):
-                arrived(src, sem.at[0, back])
-                to(src, dst, sem.at[1, line + back], sem.at[0, line + back], lm=mate())
+            arrived(line_chunk(step, h, back), wt_sems.at[h, back])
+            send_line(step, h, back, line + back, lm=mate())
 
         def product(j, low):
             vectors = [wt[step, slot, h] for slot in range(low, low + line)]
@@ -312,8 +350,7 @@
         for j in parts():
             side_acc[h, j] = product(j, 0)
         for slot in range(line, members):
-            for ref, sem in line_chunk(step, h, slot):
-                arrived(ref, sem.at[0, slot])
+            arrived(line_chunk(step, h, slot), wt_sems.at[h, slot])
         rows = stats[step - 1, h, 0]
         for slot in range(1, members):
             rows = rows + stats[step - 1, h, slot]
@@ -321,8 +358,7 @@
         for j in range(1, groups):
             to(
                 follow_out.at[step - 1, h], follow_in.at[step - 1, h, groups - j],
-                grp_sems.at[step, h, 2, 1, j], grp_sems.at[step, h, 2, 0, groups - j],
-                grp=group(j),
+                ("follow", sent_sems.at[3]), grp_sems.at[h, 2, groups - j], grp=group(j),
             )
         totals = column(rows[0:1, :])[0:hv]
         for j in parts():
@@ -341,7 +377,7 @@
         if step == 0 and h == 0:
             said = [lead_out[0]]
             for j in range(1, groups):
-                arrived(lead_in.at[j], lead_sems.at[0, 0, j])
+                arrived(lead_in.at[j], lead_sems.at[0, j])
                 said.append(lead_in[j])
             all_weight = sum(s[1:2, 0:1] for s in said)
             mean_row = sum(s[0:1, 0:part] * (s[1:2, 0:1] / all_weight) for s in said)
@@ -349,7 +385,7 @@
             for j in range(1, groups):
                 to(
                     mean_all.at[0], mean_all.at[groups - j],
-                    lead_sems.at[1, 1, j], lead_sems.at[1, 0, groups - j], grp=group(j),
+                    ("mean", sent_sems.at[4]), lead_sems.at[1, groups - j], grp=group(j),
                 )
             shared["gaps"] = flat([s[0:1, 0:part] - mean_row for s in said], groups)
             shared["totals"] = [
@@ -361,7 +397,7 @@
         else:
             said = [follow_out[step - 1, h]]
             for j in range(1, groups):
-                arrived(follow_in.at[step - 1, h, j], grp_sems.at[step, h, 2, 0, j])
+                arrived(follow_in.at[step - 1, h, j], grp_sems.at[h, 2, j])
                 said.append(follow_in[step - 1, h, j])
             totals = [s[0:1, :] for s in said]
             factor = column(
@@ -373,7 +409,7 @@
         )[0:hv]
         summed = side_acc[h, 0] + correction
         for j in range(1, groups):
-            arrived(side_in.at[step, h, j], grp_sems.at[step, h, 0, 0, j])
+            arrived(side_in.at[step, h, j], grp_sems.at[h, 0, j])
             summed = summed + side_in[step, h, j].astype(F32)
         if factor is not None:
             summed = summed * factor
@@ -381,8 +417,7 @@
         for j in range(1, groups):
             to(
                 side_b.at[step, h, 0], side_b.at[step, h, groups - j],
-                grp_sems.at[step, h, 1, 1, j], grp_sems.at[step, h, 1, 0, groups - j],
-                grp=group(j),
+                ("gather", sent_sems.at[5]), grp_sems.at[h, 1, groups - j], grp=group(j),
             )
 
     wide = 2 if line % 2 == 0 else 1
@@ -390,12 +425,12 @@
     def make_image(step, h):
         if step == 0 and h == 0:
             for j in range(1, groups):
-                arrived(mean_all.at[j], lead_sems.at[1, 0, j])
+                arrived(mean_all.at[j], lead_sems.at[1, j])
         weighed = jnp.zeros((hv, part), F32)
         blocks = []
         for j in range(groups):
             if j:
-                arrived(side_b.at[step, h, j], grp_sems.at[step, h, 1, 0, j])
+                arrived(side_b.at[step, h, j], grp_sems.at[h, 1, j])
             blocks.append(side_b[step, h, j])
             weighed = weighed + blocks[j].astype(F32) * mean_all[j, 0:1, :]
         shift = jnp.sum(weighed, axis=1, keepdims=True)
@@ -413,13 +448,13 @@
                 image_out[step, h, k] = pieces[i].astype(BF16)
                 to(
                     image_out.at[step, h, k], pair_in.at[step, h, k],
-                    img_sems.at[step, h, 0, 1, k], img_sems.at[step, h, 0, 0, k], lm=mate(),
+                    ("pair", sent_sems.at[6]), img_sems.at[h, 0, k], lm=mate(),
                 )
         for start in starts:
             pieces = product(start)
             for i in reversed(range(wide)):
                 k = start + i
-                arrived(pair_in.at[step, h, k], img_sems.at[step, h, 0, 0, k])
+                arrived(pair_in.at[step, h, k], img_sems.at[h, 0, k])
                 mine = pieces[i] + pair_in[step, h, k].astype(F32)
                 if k == 0:
                     held[h] = mine
@@ -427,14 +462,13 @@
                 line_out[step, h, k] = mine.astype(BF16)
                 to(
                     line_out.at[step, h, k], line_in.at[step, h, line - k],
-                    img_sems.at[step, h, 1, 1, k], img_sems.at[step, h, 1, 0, line - k],
-                    lm=along(k),
+                    ("sum", sent_sems.at[7]), img_sems.at[h, 1, line - k], lm=along(k),
                 )
 
     def end_image(step, h):
         image = held[h]
         for k in order:
-            arrived(line_in.at[step, h, line - k], img_sems.at[step, h, 1, 0, line - k])
+            arrived(line_in.at[step, h, line - k], img_sems.at[h, 1, line - k])
             image = image + line_in[step, h, line - k].astype(F32)
         image = weight_row * image
         square = jnp.sum(image * image, axis=1, keepdims=True)
@@ -446,12 +480,9 @@
         rows = stat_rows([jnp.sum(full, axis=1, keepdims=True), square])
         stats[step, h, 0] = jnp.zeros((8, 128), F32)
         stats[step, h, 0, :, 0:hv] = rows
-        own_chunk = line_chunk(step + 1, h, 0)
-        for (src, sem), (dst, _) in zip(own_chunk, line_chunk(step + 1, h, line)):
-            to(src, dst, sem.at[1, 0], sem.at[0, line], lm=mate())
+        send_line(step + 1, h, 0, line, lm=mate())
         for k in order:
-            for (src, sem), (dst, _) in zip(own_chunk, line_chunk(step + 1, h, line - k)):
-                to(src, dst, sem.at[1, k], sem.at[0, line - k], lm=along(k))
+            send_line(step + 1, h, 0, line - k, lm=along(k))
         return square
 
     shared = {}
@@ -473,29 +504,30 @@
     for k in range(1, members):
         back = members - k
         to(
-            norms.at[0], norms.at[back], norm_sems.at[1, k], norm_sems.at[0, back],
+            norms.at[0], norms.at[back], ("norm", sent_sems.at[8]), norm_sems.at[back],
             lm=(me_l + k) % members,
         )
     for k in range(1, members):
-        arrived(norms.at[k], norm_sems.at[0, k])
+        arrived(norms.at[k], norm_sems.at[k])
         square = square + norms[k, 0:1, :]
     group_norms[0] = jnp.broadcast_to(square, norms.shape[1:])
     for j in range(1, groups):
         back = groups - j
         to(
             group_norms.at[0], group_norms.at[back],
-            norm_sems.at[1, members + j], norm_sems.at[0, members + back], grp=group(j),
+            ("norm", sent_sems.at[8]), norm_sems.at[members + back], grp=group(j),
         )
     for j in range(1, groups):
-        arrived(group_norms.at[j], norm_sems.at[0, members + j])
+        arrived(group_norms.at[j], norm_sems.at[members + j])
         square = square + group_norms[j, 0:1, :]
     image = jnp.transpose(jnp.concatenate([held[h] for h in range(HALVES)], axis=0))
     out_ref[...] = image / jnp.sqrt(square / total_rows + 1e-06)
-    for when, copy in sends:
+    for when, sem, total in sends.values():
+        wait = waiter(bytes_of(total), sem).wait_send
         if when is None:
-            copy.wait_send()
+            wait()
         else:
-            pl.when(when)(copy.wait_send)
+            pl.when(when)(wait)
 
 
 def local(groups, members, embeddings, landmarks, start_vectors, row_weight, spread):
@@ -513,9 +545,13 @@
     return pl.pallas_call(
         functools.partial(kernel, groups, members),
         out_shape=jax.ShapeDtypeStruct((own, vecs), F32),
-        in_specs=[pl.BlockSpec(memory_space=pltpu.SMEM), vmem, pl.BlockSpec(memory_space=pl.ANY), vmem, vmem],
+        in_specs=[pl.BlockSpec(memory_space=pl.ANY)] * 5,
         out_specs=vmem,
         scratch_shapes=[
+            pltpu.SMEM((1,), F32),
+            pltpu.VMEM((own, width), BF16),
+            pltpu.VMEM((own, vecs), F32),
+            pltpu.VMEM((1, own), F32),
             pltpu.VMEM((marks, width), BF16),
             pltpu.VMEM((marks, width), BF16),
             pltpu.VMEM((marks, rows), BF16),
@@ -542,13 +578,16 @@
             pltpu.VMEM((HALVES, hv, own), F32),
             pltpu.VMEM((members, 8, vecs), F32),
             pltpu.VMEM((groups, 8, vecs), F32),
-            dma((4, 3, members + 4)),
-            dma((ITERS - 1, HALVES, 2, 2, members)),
-            dma((2, 2, groups)),
-            dma((ITERS, HALVES, 3, 2, groups)),
-            dma((ITERS, HALVES, 2, 2, line)),
-            dma((2, members + groups)),
+            dma((3, members)),
+            dma((5 + line,)),
+            dma((HALVES, members)),
+            dma((2, groups)),
+            dma((HALVES, 3, groups)),
+            dma((HALVES, 2, line)),
+            dma((members + groups,)),
+            dma((9,)),
             dma((groups,)),
+            dma((4,)),
         ],
         compiler_params=pltpu.CompilerParams(
             collective_id=0, has_side_effects=True, vmem_limit_bytes=62 * 2**20

time: 96.1 us -> 93.2 us (0.970)
  Pallas kernels: 93.7 us -> 90.8 us
    pallas_call x1, Pallas kernels: 93.7 us -> 90.8 us  [local(): pl.pallas_call(functools.partial(kernel, groups, members), out_shape=jax....]
where the time goes in v2:
time: 93.2 us; the launch traced here: 93 us
  Pallas kernels  90.8 us (97%)
  local copies, waits for them, and re-layouts  1.57 us (2%)
    pallas_call x1, Pallas kernels, local(): pl.pallas_call(functools.partial(kernel, groups, members), out_shape=jax....  90.8 us

profile of v2, /device:TPU:0, one launch (start us, length us, event | category | flops | bytes accessed | tf_op | source)
XLA Modules:
  0.0 93.0 jit_solution(9614381436005424643)
XLA Ops:
  0.7 90.8 %shard_map.55 = f32[256,128]{1,0:T(8,128)} custom-call(f32[1]{0:T(128)S(6)} %copy.7.spread_hbm, bf16[256,512]{1,0:T(8,128)(2,1)} %emb_hbm.1, bf16[2048,512]{1,0:T(8,128)(2,1)} %marks_ref.1, f32[256,128]{1,0:T(8,128)} %vec_hbm.1, f32[1,256]{1,0:T(1,128)} %bitcast.1), custom_call_target="tpu_custom_call" | custom-call | tf_op jit(solution)/shard_map/pallas_call | solution.py:545
  91.5 1.6 %copy.8 = f32[256,128]{1,0:T(8,128)} copy(f32[256,128]{1,0:T(8,128)} %shard_map.55) | data formatting | bytes 262144

commit v3 on v2

--- a/solution.py
+++ b/solution.py
@@ -10,6 +10,7 @@
 
 ITERS = 2
 HALVES = 2
+SUBS = 2
 F32 = jnp.float32
 BF16 = jnp.bfloat16
 BUILD = 1024
@@ -47,7 +48,7 @@
             if d == 1:
                 key = 1 if ahead <= behind else 2
             elif d == 2:
-                key = 0 if behind else 3
+                key = 0 if behind else line + 1
             else:
                 key = d + 1
             found.append((key, d, from_left))
@@ -58,7 +59,7 @@
     groups, members, spread_hbm, emb_hbm, marks_ref, vec_hbm, weight_hbm, out_ref,
     spread_ref, emb_ref, vec_ref, weight_ref, marks_in, marks_unit, kern_t, unit, wt, first_stats, stats, side, means, mean_rows,
     mean_all, side_out, side_in, side_acc, lead_out, lead_in, follow_out, follow_in,
-    side_b, image_out, pair_in, line_out, line_in, held, norms, group_norms,
+    side_b, image_out, pair_in, line_out, line_in, held, norms, gauge,
     row_sems, own_sems, wt_sems, lead_sems, grp_sems, img_sems, norm_sems, sent_sems,
     mark_sems, in_sems,
 ):
@@ -74,6 +75,7 @@
     z = me_l // 2
     c = me_l % 2
     half = own // 2
+    cut = part // SUBS
     sends = {}
 
     def size(ref):
@@ -94,6 +96,8 @@
 
     def bytes_of(total):
         unit = 16 * 128 * 2
+        if total % unit:
+            return gauge.at[pl.ds(0, total // 512)]
         blocks = total // unit
         across = 1
         while blocks % across or blocks // across > marks // 16:
@@ -160,37 +164,6 @@
             wide = jnp.where(lane == i, col, wide)
         return jnp.transpose(wide)[0:8, :]
 
-    pl.semaphore_wait(barrier, members - 1 + groups - 1)
-
-    def chunk(slot):
-        return [
-            ([unit.at[slot, pl.ds(0, half), :]], row_sems.at[0]),
-            ([unit.at[slot, pl.ds(half, half), :]], row_sems.at[1]),
-            ([wt.at[0, slot], first_stats.at[slot]], row_sems.at[2]),
-        ]
-
-    def send(sources, targets, name, sem, slot, when=None, **device):
-        for (srcs, _), (dsts, recv) in zip(sources, targets):
-            for src, dst in zip(srcs, dsts):
-                to(src, dst, (name, sem), recv.at[slot], when, **device)
-
-    def send_own(low, high):
-        def pieces(slot):
-            return chunk(slot)[low:high]
-
-        send(pieces(0), pieces(line), "mate", own_sems.at[0], line, lm=mate())
-        for d in (2, 1):
-            if d < line:
-                for right in (1, 0):
-                    slot = line - d if right else d
-                    send(
-                        pieces(0), pieces(slot), f"own {d} {right}",
-                        own_sems.at[2 * d + right - 1], slot,
-                        when=z < line - d if right else z >= d,
-                        lm=(z + d if right else z + line - d) % line * 2 + c,
-                    )
-
-    send_own(0, 2)
     for copy in inputs[1:]:
         copy.wait()
     gamma = spread_ref[0]
@@ -204,7 +177,37 @@
         first_stats[0, 1 + h : 2 + h, 0:hv] = stat_rows(
             [jnp.sum(piece, axis=1, keepdims=True)]
         )[0:1, :]
-    send_own(2, 3)
+    pl.semaphore_wait(barrier, members - 1 + groups - 1)
+
+    def chunk(slot):
+        return [
+            ([wt.at[0, slot], first_stats.at[slot]], row_sems.at[0]),
+            ([unit.at[slot, pl.ds(0, half), :]], row_sems.at[1]),
+            ([unit.at[slot, pl.ds(half, half), :]], row_sems.at[2]),
+        ]
+
+    def send(sources, targets, name, sem, slot, when=None, **device):
+        for (srcs, _), (dsts, recv) in zip(sources, targets):
+            for src, dst in zip(srcs, dsts):
+                to(src, dst, (name, sem), recv.at[slot], when, **device)
+
+    def send_own():
+        send(chunk(0), chunk(line), "mate", own_sems.at[0], line, lm=mate())
+        for d, early in ((2, True), (1, False), (2, False)):
+            if d < line:
+                for right in (1, 0):
+                    slot = line - d if right else d
+                    goes = z < line - d if right else z >= d
+                    relayed = z < line - 3 if right else z >= 3
+                    if d == 2:
+                        goes = relayed if early else goes & ~relayed
+                    send(
+                        chunk(0), chunk(slot), f"own {d} {right} {early}",
+                        own_sems.at[2 * d + right - 1], slot, when=goes,
+                        lm=(z + d if right else z + line - d) % line * 2 + c,
+                    )
+
+    send_own()
 
     mark_tile = tile(part, 256)
 
@@ -227,7 +230,7 @@
             found = jnp.where(z == position, jnp.int32(table[position]), found)
         return found
 
-    def relay(t):
+    def relay(t, low=0, high=3):
         plan = [visits(position, line)[t] for position in range(line)]
         slot = at_z([line - d if left else d for d, left in plan])
         left = at_z([int(left) for _, left in plan]) == 1
@@ -236,29 +239,34 @@
             for position, (d, left) in enumerate(plan)
         ]) == 1
         follow = jnp.where(more, jnp.where(left, slot - 1, slot + 1), slot)
-        for source, target in zip(chunk(slot), chunk(follow)):
+        for source, target in zip(chunk(slot)[low:high], chunk(follow)[low:high]):
             arrived(source[0], source[1].at[slot])
             send(
                 [source], [target], f"relay {t}", own_sems.at[5 + t], follow, when=more,
                 lm=jnp.where(left, z + 1, z - 1 + line) % line * 2 + c,
             )
-        send(chunk(slot), chunk(line + slot), "mate", own_sems.at[0], line + slot, lm=mate())
+        send(
+            chunk(slot)[low:high], chunk(line + slot)[low:high], "mate", own_sems.at[0],
+            line + slot, lm=mate(),
+        )
         return slot
 
-    def build(slot, first=False):
-        here = pl.ds(pl.multiple_of(slot * own, own), own)
+    def build(slot, low=0, high=own):
+        count = high - low
+        here = pl.ds(pl.multiple_of(slot * own + low, math.gcd(own, 128)), count)
 
         def visit(i, carry):
             at = rows_at(i, build_tile)
-            tall = jnp.exp(gamma * nt(marks_unit[at, :], unit[slot]))
+            tall = jnp.exp(gamma * nt(marks_unit[at, :], unit[slot, low:high, :]))
             tall_b = tall.astype(BF16)
             kern_t[at, here] = tall_b
-            scaled = tall * first_stats[slot, 0:1, 0:own]
+            scaled = tall * first_stats[slot, 0:1, low:high]
             fold = scaled[:, 0:128]
-            for piece in range(1, own // 128):
+            for piece in range(1, count // 128):
                 fold = fold + scaled[:, piece * 128 : (piece + 1) * 128]
-            product = nt(tall_b, wt[0, slot].reshape(vecs, own))
-            if first:
+            vectors = wt[0, slot, :, :, low:high].reshape(vecs, count)
+            product = nt(tall_b, vectors)
+            if isinstance(slot, int) and slot == 0:
                 means[at, :] = fold
                 side[at, :] = product
             else:
@@ -268,32 +276,41 @@
 
         lax.fori_loop(0, marks // build_tile, visit, 0)
 
+    def await_mate(slot, low=0, high=3):
+        for refs, sem in chunk(slot)[low:high]:
+            arrived(refs, sem.at[slot])
+
     build_tile = tile(marks, BUILD)
-    build(0, True)
-    def await_mate(slot):
-        for refs, sem in chunk(slot):
-            arrived(refs, sem.at[slot])
-
+    build(0)
     await_mate(line)
     build(line)
-    for t in range(line - 1):
+    for t in range(line - 2):
         slot = relay(t)
         build(slot)
         await_mate(line + slot)
         build(line + slot)
+    if line > 1:
+        slot = relay(line - 2, 0, 2)
+        build(slot, 0, half)
+        relay(line - 2, 2, 3)
+        await_mate(line + slot, 0, 2)
+        build(line + slot, 0, half)
+        build(slot, half, own)
+        await_mate(line + slot, 2, 3)
+        build(line + slot, half, own)
 
     def parts():
         return [*range(1, groups), 0]
 
-    def send_side(step, h, j):
+    def send_side(step, h, j, sub):
         to(
-            side_out.at[step, h, j], side_in.at[step, h, groups - j],
-            ("side", sent_sems.at[0]), grp_sems.at[h, 0, groups - j], grp=group(j),
+            side_out.at[step, h, sub, j], side_in.at[step, h, sub, groups - j],
+            ("side", sent_sems.at[0]), grp_sems.at[h, sub, groups - j], grp=group(j),
         )
 
     def first_side():
         weight_sum = jnp.zeros((1, 1), F32)
-        rows = jnp.zeros((8, 128), F32)
+        rows = jnp.zeros((2 + HALVES, 128), F32)
         for slot in range(members):
             weight_sum = weight_sum + jnp.sum(
                 first_stats[slot, 0:1, 0:own], axis=1, keepdims=True
@@ -317,15 +334,17 @@
                 )
             for h in range(HALVES):
                 piece = block[h * hv : (h + 1) * hv, :]
-                if j:
-                    side_out[0, h, j] = piece.astype(BF16)
-                    if h == 0:
-                        send_side(0, h, j)
-                else:
+                if j == 0:
                     side_acc[h, 0] = piece
-        for h in range(1, HALVES):
-            for j in range(1, groups):
-                send_side(0, h, j)
+                    continue
+                for sub in range(SUBS):
+                    side_out[0, h, sub, j] = piece[:, sub * cut : (sub + 1) * cut].astype(BF16)
+                if h == 0:
+                    send_side(0, h, j, 0)
+        for h in range(HALVES):
+            for sub in range(h == 0, SUBS):
+                for j in range(1, groups):
+                    send_side(0, h, j, sub)
 
     def line_chunk(step, h, slot):
         return [wt.at[step, slot, h], stats.at[step - 1, h, slot]]
@@ -340,11 +359,15 @@
             arrived(line_chunk(step, h, back), wt_sems.at[h, back])
             send_line(step, h, back, line + back, lm=mate())
 
-        def product(j, low):
+        def product(j, low, sub=None):
             vectors = [wt[step, slot, h] for slot in range(low, low + line)]
+            first = j * part + (sub or 0) * cut
             return nt(
                 jnp.concatenate(vectors, axis=1),
-                kern_t[j * part : (j + 1) * part, low * own : (low + line) * own],
+                kern_t[
+                    first : first + (part if sub is None else cut),
+                    low * own : (low + line) * own,
+                ],
             )
 
         for j in parts():
@@ -358,16 +381,19 @@
         for j in range(1, groups):
             to(
                 follow_out.at[step - 1, h], follow_in.at[step - 1, h, groups - j],
-                ("follow", sent_sems.at[3]), grp_sems.at[h, 2, groups - j], grp=group(j),
+                ("follow", sent_sems.at[3]), grp_sems.at[h, 2 * SUBS, groups - j], grp=group(j),
             )
         totals = column(rows[0:1, :])[0:hv]
-        for j in parts():
-            block = side_acc[h, j] + product(j, line) - totals * mean_rows[j, 0:1, :]
-            if j:
-                side_out[step, h, j] = block.astype(BF16)
-                send_side(step, h, j)
-            else:
-                side_acc[h, 0] = block
+        for sub in range(SUBS):
+            at = slice(sub * cut, (sub + 1) * cut)
+            for j in parts():
+                block = side_acc[h, j, :, at] + product(j, line, sub)
+                block = block - totals * mean_rows[j, 0:1, at]
+                if j:
+                    side_out[step, h, sub, j] = block.astype(BF16)
+                    send_side(step, h, j, sub)
+                else:
+                    side_acc[h, 0, :, at] = block
 
     def flat(rows, height):
         pad = -height % 8
@@ -381,7 +407,7 @@
                 said.append(lead_in[j])
             all_weight = sum(s[1:2, 0:1] for s in said)
             mean_row = sum(s[0:1, 0:part] * (s[1:2, 0:1] / all_weight) for s in said)
-            mean_all[0] = jnp.broadcast_to(mean_row, (8, part))
+            mean_all[0] = mean_row
             for j in range(1, groups):
                 to(
                     mean_all.at[0], mean_all.at[groups - j],
@@ -397,7 +423,7 @@
         else:
             said = [follow_out[step - 1, h]]
             for j in range(1, groups):
-                arrived(follow_in.at[step - 1, h, j], grp_sems.at[h, 2, j])
+                arrived(follow_in.at[step - 1, h, j], grp_sems.at[h, 2 * SUBS, j])
                 said.append(follow_in[step - 1, h, j])
             totals = [s[0:1, :] for s in said]
             factor = column(
@@ -407,18 +433,21 @@
             flat(totals, groups), shared["gaps"],
             (((0,), (0,)), ((), ())), precision=HIGHEST, preferred_element_type=F32,
         )[0:hv]
-        summed = side_acc[h, 0] + correction
-        for j in range(1, groups):
-            arrived(side_in.at[step, h, j], grp_sems.at[h, 0, j])
-            summed = summed + side_in[step, h, j].astype(F32)
-        if factor is not None:
-            summed = summed * factor
-        side_b[step, h, 0] = summed.astype(BF16)
-        for j in range(1, groups):
-            to(
-                side_b.at[step, h, 0], side_b.at[step, h, groups - j],
-                ("gather", sent_sems.at[5]), grp_sems.at[h, 1, groups - j], grp=group(j),
-            )
+        for sub in range(SUBS):
+            at = slice(sub * cut, (sub + 1) * cut)
+            summed = side_acc[h, 0, :, at] + correction[:, at]
+            for j in range(1, groups):
+                arrived(side_in.at[step, h, sub, j], grp_sems.at[h, sub, j])
+                summed = summed + side_in[step, h, sub, j].astype(F32)
+            if factor is not None:
+                summed = summed * factor
+            side_b[step, h, sub, 0] = summed.astype(BF16)
+            for j in range(1, groups):
+                to(
+                    side_b.at[step, h, sub, 0], side_b.at[step, h, sub, groups - j],
+                    ("gather", sent_sems.at[5]), grp_sems.at[h, SUBS + sub, groups - j],
+                    grp=group(j),
+                )
 
     wide = 2 if line % 2 == 0 else 1
 
@@ -428,10 +457,13 @@
                 arrived(mean_all.at[j], lead_sems.at[1, j])
         weighed = jnp.zeros((hv, part), F32)
         blocks = []
+        for sub in range(SUBS):
+            for j in range(1, groups):
+                arrived(side_b.at[step, h, sub, j], grp_sems.at[h, SUBS + sub, j])
         for j in range(groups):
-            if j:
-                arrived(side_b.at[step, h, j], grp_sems.at[h, 1, j])
-            blocks.append(side_b[step, h, j])
+            blocks.append(jnp.concatenate(
+                [side_b[step, h, sub, j] for sub in range(SUBS)], axis=1
+            ))
             weighed = weighed + blocks[j].astype(F32) * mean_all[j, 0:1, :]
         shift = jnp.sum(weighed, axis=1, keepdims=True)
         whole = jnp.concatenate(blocks, axis=1)
@@ -478,8 +510,8 @@
         full = weight_row * image
         wt[step + 1, 0, h] = full.astype(BF16)
         rows = stat_rows([jnp.sum(full, axis=1, keepdims=True), square])
-        stats[step, h, 0] = jnp.zeros((8, 128), F32)
-        stats[step, h, 0, :, 0:hv] = rows
+        stats[step, h, 0] = jnp.zeros((2, 128), F32)
+        stats[step, h, 0, :, 0:hv] = rows[0:2, :]
         send_line(step + 1, h, 0, line, lm=mate())
         for k in order:
             send_line(step + 1, h, 0, line - k, lm=along(k))
@@ -500,26 +532,17 @@
         squares = [end_image(step, h) for h in range(HALVES)]
 
     square = stat_rows([jnp.concatenate(squares, axis=0)])[0:1, :]
-    norms[0] = jnp.broadcast_to(square, norms.shape[1:])
-    for k in range(1, members):
-        back = members - k
+    norms[0] = square
+    others = [(j, k) for j in range(groups) for k in range(members)][1:]
+    for j, k in others:
+        there = (groups - j) % groups * members + (members - k) % members
         to(
-            norms.at[0], norms.at[back], ("norm", sent_sems.at[8]), norm_sems.at[back],
-            lm=(me_l + k) % members,
-        )
-    for k in range(1, members):
-        arrived(norms.at[k], norm_sems.at[k])
-        square = square + norms[k, 0:1, :]
-    group_norms[0] = jnp.broadcast_to(square, norms.shape[1:])
-    for j in range(1, groups):
-        back = groups - j
-        to(
-            group_norms.at[0], group_norms.at[back],
-            ("norm", sent_sems.at[8]), norm_sems.at[members + back], grp=group(j),
-        )
-    for j in range(1, groups):
-        arrived(group_norms.at[j], norm_sems.at[members + j])
-        square = square + group_norms[j, 0:1, :]
+            norms.at[0], norms.at[there], ("norm", sent_sems.at[8]), norm_sems.at[there],
+            grp=group(j), lm=(me_l + k) % members,
+        )
+    for j, k in others:
+        arrived(norms.at[j * members + k], norm_sems.at[j * members + k])
+    square = jnp.sum(norms[:, 0, :], axis=0, keepdims=True)
     image = jnp.transpose(jnp.concatenate([held[h] for h in range(HALVES)], axis=0))
     out_ref[...] = image / jnp.sqrt(square / total_rows + 1e-06)
     for when, sem, total in sends.values():
@@ -557,34 +580,34 @@
             pltpu.VMEM((marks, rows), BF16),
             pltpu.VMEM((members, own, width), BF16),
             pltpu.VMEM((ITERS, members, HALVES, hv, own), BF16),
-            pltpu.VMEM((members, 8, wide), F32),
-            pltpu.VMEM((ITERS - 1, HALVES, members, 8, 128), F32),
+            pltpu.VMEM((members, 2 + HALVES, wide), F32),
+            pltpu.VMEM((ITERS - 1, HALVES, members, 2, 128), F32),
             pltpu.VMEM((marks, vecs), F32),
             pltpu.VMEM((marks, 128), F32),
             pltpu.VMEM((groups, 8, part), F32),
-            pltpu.VMEM((groups, 8, part), F32),
-            pltpu.VMEM((ITERS, HALVES, groups, hv, part), BF16),
-            pltpu.VMEM((ITERS, HALVES, groups, hv, part), BF16),
+            pltpu.VMEM((groups, 1, part), F32),
+            pltpu.VMEM((ITERS, HALVES, SUBS, groups, hv, part // SUBS), BF16),
+            pltpu.VMEM((ITERS, HALVES, SUBS, groups, hv, part // SUBS), BF16),
             pltpu.VMEM((HALVES, groups, hv, part), F32),
-            pltpu.VMEM((groups, 8, span), F32),
-            pltpu.VMEM((groups, 8, span), F32),
-            pltpu.VMEM((ITERS - 1, HALVES, 8, 128), F32),
-            pltpu.VMEM((ITERS - 1, HALVES, groups, 8, 128), F32),
-            pltpu.VMEM((ITERS, HALVES, groups, hv, part), BF16),
+            pltpu.VMEM((groups, 2 + HALVES, span), F32),
+            pltpu.VMEM((groups, 2 + HALVES, span), F32),
+            pltpu.VMEM((ITERS - 1, HALVES, 2, 128), F32),
+            pltpu.VMEM((ITERS - 1, HALVES, groups, 2, 128), F32),
+            pltpu.VMEM((ITERS, HALVES, SUBS, groups, hv, part // SUBS), BF16),
             pltpu.VMEM((ITERS, HALVES, line, hv, own), BF16),
             pltpu.VMEM((ITERS, HALVES, line, hv, own), BF16),
             pltpu.VMEM((ITERS, HALVES, line, hv, own), BF16),
             pltpu.VMEM((ITERS, HALVES, line, hv, own), BF16),
             pltpu.VMEM((HALVES, hv, own), F32),
-            pltpu.VMEM((members, 8, vecs), F32),
-            pltpu.VMEM((groups, 8, vecs), F32),
+            pltpu.VMEM((groups * members, 1, vecs), F32),
+            pltpu.VMEM((HALVES * members * (hv * own // 256 + 2), 1, 128), F32),
             dma((3, members)),
             dma((5 + line,)),
             dma((HALVES, members)),
             dma((2, groups)),
-            dma((HALVES, 3, groups)),
+            dma((HALVES, 2 * SUBS + 1, groups)),
             dma((HALVES, 2, line)),
-            dma((members + groups,)),
+            dma((groups * members,)),
             dma((9,)),
             dma((groups,)),
             dma((4,)),

time: 93.2 us -> 90.2 us (0.968)
  Pallas kernels: 90.8 us -> 87.8 us
    pallas_call x1, Pallas kernels: 90.8 us -> 87.8 us  [local(): pl.pallas_call(functools.partial(kernel, groups, members), out_shape=jax....]
where the time goes in v3:
time: 90.2 us; the launch traced here: 90 us
  Pallas kernels  87.8 us (97%)
  local copies, waits for them, and re-layouts  1.57 us (2%)
    pallas_call x1, Pallas kernels, local(): pl.pallas_call(functools.partial(kernel, groups, members), out_shape=jax....  87.8 us

profile of v3, /device:TPU:0, one launch (start us, length us, event | category | flops | bytes accessed | tf_op | source)
XLA Modules:
  0.0 90.0 jit_solution(7508680384087262461)
XLA Ops:
  0.7 87.8 %shard_map.55 = f32[256,128]{1,0:T(8,128)} custom-call(f32[1]{0:T(128)S(6)} %copy.7.spread_hbm, bf16[256,512]{1,0:T(8,128)(2,1)} %emb_hbm.1, bf16[2048,512]{1,0:T(8,128)(2,1)} %marks_ref.1, f32[256,128]{1,0:T(8,128)} %vec_hbm.1, f32[1,256]{1,0:T(1,128)} %bitcast.1), custom_call_target="tpu_custom_call" | custom-call | tf_op jit(solution)/shard_map/pallas_call | solution.py:568
  88.4 1.6 %copy.8 = f32[256,128]{1,0:T(8,128)} copy(f32[256,128]{1,0:T(8,128)} %shard_map.55) | data formatting | bytes 262144

commit v4 on v3

--- a/solution.py
+++ b/solution.py
@@ -10,7 +10,7 @@
 
 ITERS = 2
 HALVES = 2
-SUBS = 2
+SUBS = 1
 F32 = jnp.float32
 BF16 = jnp.bfloat16
 BUILD = 1024
@@ -292,9 +292,9 @@
     if line > 1:
         slot = relay(line - 2, 0, 2)
         build(slot, 0, half)
-        relay(line - 2, 2, 3)
         await_mate(line + slot, 0, 2)
         build(line + slot, 0, half)
+        relay(line - 2, 2, 3)
         build(slot, half, own)
         await_mate(line + slot, 2, 3)
         build(line + slot, half, own)
@@ -567,7 +567,7 @@
     dma = pltpu.SemaphoreType.DMA
     return pl.pallas_call(
         functools.partial(kernel, groups, members),
-        out_shape=jax.ShapeDtypeStruct((own, vecs), F32),
+        out_shape=pltpu.VMEM((own, vecs), F32),
         in_specs=[pl.BlockSpec(memory_space=pl.ANY)] * 5,
         out_specs=vmem,
         scratch_shapes=[

time: 90.2 us -> 85.8 us (0.951)
  Pallas kernels: 87.8 us -> 84.3 us
  local copies, waits for them, and re-layouts: 1.57 us -> 0.66 us
    pallas_call x1, Pallas kernels: 87.8 us -> 84.3 us  [local(): pl.pallas_call(functools.partial(kernel, groups, members), out_shape=pltp...]
    unnamed x1, local copies, waits for them, and re-layouts: 1.57 us -> 0.66 us
where the time goes in v4:
time: 85.8 us; the launch traced here: 85.6 us
  Pallas kernels  84.3 us (98%)
    pallas_call x1, Pallas kernels, local(): pl.pallas_call(functools.partial(kernel, groups, members), out_shape=pltp...  84.3 us

profile of v4, /device:TPU:0, one launch (start us, length us, event | category | flops | bytes accessed | tf_op | source)
XLA Modules:
  0.0 85.6 jit_solution(8547888675360710994)
XLA Ops:
  0.7 84.3 %shard_map.55 = f32[256,128]{1,0:T(8,128)S(1)} custom-call(f32[1]{0:T(128)S(6)} %copy.8.spread_hbm, bf16[256,512]{1,0:T(8,128)(2,1)} %emb_hbm.1, bf16[2048,512]{1,0:T(8,128)(2,1)} %marks_ref.1, f32[256,128]{1,0:T(8,128)} %vec_hbm.1, f32[1,256]{1,0:T(1,128)} %bitcast.1), custom_call_target="tpu_custom_call" | custom-call | tf_op jit(solution)/shard_map/pallas_call | solution.py:568
  84.9 0.7 copy.7

commit v5 on v4

--- a/solution.py
+++ b/solution.py
@@ -276,6 +276,18 @@
 
         lax.fori_loop(0, marks // build_tile, visit, 0)
 
+    def first_totals():
+        weight_sum = jnp.zeros((1, 1), F32)
+        rows = jnp.zeros((2 + HALVES, 128), F32)
+        for slot in range(members):
+            weight_sum = weight_sum + jnp.sum(
+                first_stats[slot, 0:1, 0:own], axis=1, keepdims=True
+            )
+            rows = rows + first_stats[slot, :, 0:128]
+        totals = [column(rows[1 + h : 2 + h, 0:128])[0:hv] for h in range(HALVES)]
+        totals = jnp.concatenate(totals, axis=0)
+        return weight_sum, rows, totals
+
     def await_mate(slot, low=0, high=3):
         for refs, sem in chunk(slot)[low:high]:
             arrived(refs, sem.at[slot])
@@ -293,11 +305,14 @@
         slot = relay(line - 2, 0, 2)
         build(slot, 0, half)
         await_mate(line + slot, 0, 2)
+        weight_sum, rows, totals = first_totals()
         build(line + slot, 0, half)
         relay(line - 2, 2, 3)
         build(slot, half, own)
         await_mate(line + slot, 2, 3)
         build(line + slot, half, own)
+    else:
+        weight_sum, rows, totals = first_totals()
 
     def parts():
         return [*range(1, groups), 0]
@@ -305,19 +320,10 @@
     def send_side(step, h, j, sub):
         to(
             side_out.at[step, h, sub, j], side_in.at[step, h, sub, groups - j],
-            ("side", sent_sems.at[0]), grp_sems.at[h, sub, groups - j], grp=group(j),
+            ("side", sent_sems.at[0]), grp_sems.at[h, sub], grp=group(j),
         )
 
     def first_side():
-        weight_sum = jnp.zeros((1, 1), F32)
-        rows = jnp.zeros((2 + HALVES, 128), F32)
-        for slot in range(members):
-            weight_sum = weight_sum + jnp.sum(
-                first_stats[slot, 0:1, 0:own], axis=1, keepdims=True
-            )
-            rows = rows + first_stats[slot, :, 0:128]
-        totals = [column(rows[1 + h : 2 + h, 0:128])[0:hv] for h in range(HALVES)]
-        totals = jnp.concatenate(totals, axis=0)
         for j in parts():
             span = pl.ds(j * part, part)
             mean = jnp.sum(jnp.transpose(means[span, :]), axis=0, keepdims=True) / weight_sum
@@ -330,7 +336,7 @@
             if j:
                 to(
                     lead_out.at[j], lead_in.at[groups - j],
-                    ("lead", sent_sems.at[1]), lead_sems.at[0, groups - j], grp=group(j),
+                    ("lead", sent_sems.at[1]), lead_sems.at[0], grp=group(j),
                 )
             for h in range(HALVES):
                 piece = block[h * hv : (h + 1) * hv, :]
@@ -351,7 +357,7 @@
 
     def send_line(step, h, source, target, **device):
         for src, dst in zip(line_chunk(step, h, source), line_chunk(step, h, target)):
-            to(src, dst, ("line", sent_sems.at[2]), wt_sems.at[h, target], **device)
+            to(src, dst, ("line", sent_sems.at[2]), wt_sems.at[h, min(target, line)], **device)
 
     def next_side(step, h):
         for k in order:
@@ -372,8 +378,8 @@
 
         for j in parts():
             side_acc[h, j] = product(j, 0)
-        for slot in range(line, members):
-            arrived(line_chunk(step, h, slot), wt_sems.at[h, slot])
+        mates = [line_chunk(step, h, slot) for slot in range(line, members)]
+        arrived([ref for pair in mates for ref in pair], wt_sems.at[h, line])
         rows = stats[step - 1, h, 0]
         for slot in range(1, members):
             rows = rows + stats[step - 1, h, slot]
@@ -381,7 +387,7 @@
         for j in range(1, groups):
             to(
                 follow_out.at[step - 1, h], follow_in.at[step - 1, h, groups - j],
-                ("follow", sent_sems.at[3]), grp_sems.at[h, 2 * SUBS, groups - j], grp=group(j),
+                ("follow", sent_sems.at[3]), grp_sems.at[h, 2 * SUBS], grp=group(j),
             )
         totals = column(rows[0:1, :])[0:hv]
         for sub in range(SUBS):
@@ -402,8 +408,8 @@
     def gather_side(step, h, shared):
         if step == 0 and h == 0:
             said = [lead_out[0]]
+            arrived([lead_in.at[j] for j in range(1, groups)], lead_sems.at[0])
             for j in range(1, groups):
-                arrived(lead_in.at[j], lead_sems.at[0, j])
                 said.append(lead_in[j])
             all_weight = sum(s[1:2, 0:1] for s in said)
             mean_row = sum(s[0:1, 0:part] * (s[1:2, 0:1] / all_weight) for s in said)
@@ -411,7 +417,7 @@
             for j in range(1, groups):
                 to(
                     mean_all.at[0], mean_all.at[groups - j],
-                    ("mean", sent_sems.at[4]), lead_sems.at[1, groups - j], grp=group(j),
+                    ("mean", sent_sems.at[4]), lead_sems.at[1], grp=group(j),
                 )
             shared["gaps"] = flat([s[0:1, 0:part] - mean_row for s in said], groups)
             shared["totals"] = [
@@ -422,8 +428,11 @@
             totals = shared["totals"][h]
         else:
             said = [follow_out[step - 1, h]]
+            arrived(
+                [follow_in.at[step - 1, h, j] for j in range(1, groups)],
+                grp_sems.at[h, 2 * SUBS],
+            )
             for j in range(1, groups):
-                arrived(follow_in.at[step - 1, h, j], grp_sems.at[h, 2 * SUBS, j])
                 said.append(follow_in[step - 1, h, j])
             totals = [s[0:1, :] for s in said]
             factor = column(
@@ -436,8 +445,10 @@
         for sub in range(SUBS):
             at = slice(sub * cut, (sub + 1) * cut)
             summed = side_acc[h, 0, :, at] + correction[:, at]
+            arrived(
+                [side_in.at[step, h, sub, j] for j in range(1, groups)], grp_sems.at[h, sub]
+            )
             for j in range(1, groups):
-                arrived(side_in.at[step, h, sub, j], grp_sems.at[h, sub, j])
                 summed = summed + side_in[step, h, sub, j].astype(F32)
             if factor is not None:
                 summed = summed * factor
@@ -445,7 +456,7 @@
             for j in range(1, groups):
                 to(
                     side_b.at[step, h, sub, 0], side_b.at[step, h, sub, groups - j],
-                    ("gather", sent_sems.at[5]), grp_sems.at[h, SUBS + sub, groups - j],
+                    ("gather", sent_sems.at[5]), grp_sems.at[h, SUBS + sub],
                     grp=group(j),
                 )
 
@@ -453,13 +464,14 @@
 
     def make_image(step, h):
         if step == 0 and h == 0:
-            for j in range(1, groups):
-                arrived(mean_all.at[j], lead_sems.at[1, j])
+            arrived([mean_all.at[j] for j in range(1, groups)], lead_sems.at[1])
         weighed = jnp.zeros((hv, part), F32)
         blocks = []
         for sub in range(SUBS):
-            for j in range(1, groups):
-                arrived(side_b.at[step, h, sub, j], grp_sems.at[h, SUBS + sub, j])
+            arrived(
+                [side_b.at[step, h, sub, j] for j in range(1, groups)],
+                grp_sems.at[h, SUBS + sub],
+            )
         for j in range(groups):
             blocks.append(jnp.concatenate(
                 [side_b[step, h, sub, j] for sub in range(SUBS)], axis=1
@@ -480,13 +492,13 @@
                 image_out[step, h, k] = pieces[i].astype(BF16)
                 to(
                     image_out.at[step, h, k], pair_in.at[step, h, k],
-                    ("pair", sent_sems.at[6]), img_sems.at[h, 0, k], lm=mate(),
+                    ("pair", sent_sems.at[6]), img_sems.at[h, k], lm=mate(),
                 )
         for start in starts:
             pieces = product(start)
             for i in reversed(range(wide)):
                 k = start + i
-                arrived(pair_in.at[step, h, k], img_sems.at[h, 0, k])
+                arrived(pair_in.at[step, h, k], img_sems.at[h, k])
                 mine = pieces[i] + pair_in[step, h, k].astype(F32)
                 if k == 0:
                     held[h] = mine
@@ -494,13 +506,13 @@
                 line_out[step, h, k] = mine.astype(BF16)
                 to(
                     line_out.at[step, h, k], line_in.at[step, h, line - k],
-                    ("sum", sent_sems.at[7]), img_sems.at[h, 1, line - k], lm=along(k),
+                    ("sum", sent_sems.at[7]), img_sems.at[h, line], lm=along(k),
                 )
 
     def end_image(step, h):
         image = held[h]
+        arrived([line_in.at[step, h, k] for k in order], img_sems.at[h, line])
         for k in order:
-            arrived(line_in.at[step, h, line - k], img_sems.at[h, 1, line - k])
             image = image + line_in[step, h, line - k].astype(F32)
         image = weight_row * image
         square = jnp.sum(image * image, axis=1, keepdims=True)
@@ -537,11 +549,10 @@
     for j, k in others:
         there = (groups - j) % groups * members + (members - k) % members
         to(
-            norms.at[0], norms.at[there], ("norm", sent_sems.at[8]), norm_sems.at[there],
+            norms.at[0], norms.at[there], ("norm", sent_sems.at[8]), norm_sems.at[0],
             grp=group(j), lm=(me_l + k) % members,
         )
-    for j, k in others:
-        arrived(norms.at[j * members + k], norm_sems.at[j * members + k])
+    arrived([norms.at[j * members + k] for j, k in others], norm_sems.at[0])
     square = jnp.sum(norms[:, 0, :], axis=0, keepdims=True)
     image = jnp.transpose(jnp.concatenate([held[h] for h in range(HALVES)], axis=0))
     out_ref[...] = image / jnp.sqrt(square / total_rows + 1e-06)
@@ -603,11 +614,11 @@
             pltpu.VMEM((HALVES * members * (hv * own // 256 + 2), 1, 128), F32),
             dma((3, members)),
             dma((5 + line,)),
-            dma((HALVES, members)),
-            dma((2, groups)),
-            dma((HALVES, 2 * SUBS + 1, groups)),
-            dma((HALVES, 2, line)),
-            dma((groups * members,)),
+            dma((HALVES, line + 1)),
+            dma((2,)),
+            dma((HALVES, 2 * SUBS + 1)),
+            dma((HALVES, line + 1)),
+            dma((1,)),
             dma((9,)),
             dma((groups,)),
             dma((4,)),

time: 85.8 us -> 85.1 us (level)
  no operation moved by 1% of the time
where the time goes in v5:
time: 85.1 us; the launch traced here: 84.9 us
  Pallas kernels  83.6 us (98%)
    pallas_call x1, Pallas kernels, local(): pl.pallas_call(functools.partial(kernel, groups, members), out_shape=pltp...  83.6 us

profile of v5, /device:TPU:0, one launch (start us, length us, event | category | flops | bytes accessed | tf_op | source)
XLA Modules:
  0.0 84.9 jit_solution(2829335349488780105)
XLA Ops:
  0.7 83.6 %shard_map.55 = f32[256,128]{1,0:T(8,128)S(1)} custom-call(f32[1]{0:T(128)S(6)} %copy.8.spread_hbm, bf16[256,512]{1,0:T(8,128)(2,1)} %emb_hbm.1, bf16[2048,512]{1,0:T(8,128)(2,1)} %marks_ref.1, f32[256,128]{1,0:T(8,128)} %vec_hbm.1, f32[1,256]{1,0:T(1,128)} %bitcast.1), custom_call_target="tpu_custom_call" | custom-call | tf_op jit(solution)/shard_map/pallas_call | solution.py:579
  84.3 0.7 copy.7
